TPU v7x, 256 devices: a whole 4x4x8 slice. The times are simulated.
256 devices in a mesh: depth: 4 (over x), row: 16 (over z, core), col: 4 (over y).
Axes of the slice: x: 4, y: 4, z: 8, core: 2. Of those that a mesh axis runs over, the one named last changes fastest.
Arguments:
- tokens: float32 [8192, 8192], P(('depth', 'col'), 'row'), may hold values from -16 to 16
- w_query: float32 [8192, 4096], P('row', 'col'), may hold values from -0.0625 to 0.0625
- w_key: float32 [8192, 512], P('row', 'col'), may hold values from -0.0625 to 0.0625
- w_value: float32 [8192, 512], P('row', 'col'), may hold values from -0.0625 to 0.0625
- w_out: float32 [4096, 8192], P('col', 'row'), may hold values from -0.09375 to 0.09375
Outputs:
- mixed: float32 [8192, 8192], P(('depth', 'col'), 'row')
All inputs are finite; a program needn't handle non-finite values.
Results may differ from a plain program's by a relative error of at most 0.0003.
Values sent between devices are 32-bit elements; how exact they have to be, the bound alone decides.
A program may use at most 64 MiB of HBM per device.

v0:
```python
import math

import jax
import numpy as np
import jax.numpy as jnp
from jax import lax
from jax.sharding import PartitionSpec as P

QUERY_HEADS = 32
KEY_VALUE_HEADS = 4
HEAD_SIZE_DIM = 128


def start_state(query_rows, kv_width):
    count_of_heads = kv_width // HEAD_SIZE_DIM
    queries_per_group = QUERY_HEADS // KEY_VALUE_HEADS
    count_of_rows = query_rows.shape[0]
    running_max = jnp.full((count_of_heads, queries_per_group, count_of_rows), -1e30, jnp.float32)
    running_sum = jnp.zeros((count_of_heads, queries_per_group, count_of_rows), jnp.float32)
    weighted = jnp.zeros(
        (count_of_heads, queries_per_group, count_of_rows, HEAD_SIZE_DIM), jnp.float32
    )
    return (running_max, running_sum, weighted)


def fold_keys(query_rows, state_now, block_pair):
    highest = lax.Precision.HIGH
    running_max, running_sum, weighted = state_now
    key_block, value_block = block_pair
    count_of_heads = key_block.shape[1] // HEAD_SIZE_DIM
    count_of_rows = query_rows.shape[0]
    query_head_rows = query_rows.reshape(
        count_of_rows, count_of_heads, QUERY_HEADS // KEY_VALUE_HEADS, HEAD_SIZE_DIM
    )
    key_head_rows = key_block.reshape(-1, count_of_heads, HEAD_SIZE_DIM)
    value_head_rows = value_block.reshape(-1, count_of_heads, HEAD_SIZE_DIM)
    scores = jnp.einsum("rkgd,nkd->kgrn", query_head_rows, key_head_rows, precision=highest) * (
        1.0 / math.sqrt(HEAD_SIZE_DIM)
    )
    newest = jnp.maximum(running_max, jnp.max(scores, axis=-1))
    weights = jnp.exp(scores - newest[..., None])
    running_sum = jnp.sum(weights, axis=-1)
    weighted = jnp.einsum("kgrn,nkd->kgrd", weights, value_head_rows, precision=highest)
    return (newest, running_sum, weighted)


def finish(state_now):
    running_max, running_sum, weighted = state_now
    attention_output = weighted / running_sum[..., None]
    count_of_heads, queries_per_group, count_of_rows, head_size = attention_output.shape
    return attention_output.transpose(2, 0, 1, 3).reshape(
        count_of_rows, count_of_heads * queries_per_group * head_size
    )


def on_device(tokens, w_query, w_key, w_value, w_out):
    highest = lax.Precision.HIGH
    gathered = lax.all_gather(tokens, "col", axis=0, tiled=True)
    q_width = w_query.shape[1]
    kv_width = w_key.shape[1]

    def product(weight):
        return jnp.dot(gathered, weight, preferred_element_type=jnp.float32, precision=highest)

    partial = jnp.concatenate([product(w_query), product(w_key), product(w_value)], axis=1)
    on_chip = lax.psum_scatter(partial, "rc", scatter_dimension=0, tiled=True)
    joined = lax.psum_scatter(on_chip, "rz", scatter_dimension=0, tiled=True)
    query_rows = joined[:, :q_width]
    local_kv = joined[:, q_width:]
    all_kv = lax.all_gather(lax.all_gather(local_kv, "rz", axis=0, tiled=True), "rc", axis=0, tiled=True)
    state_end = fold_keys(
        query_rows,
        start_state(query_rows, kv_width),
        (all_kv[:, :kv_width], all_kv[:, kv_width:]),
    )
    attention_output = finish(state_end)
    set_attended = lax.all_gather(
        lax.all_gather(attention_output, "rz", axis=0, tiled=True), "rc", axis=0, tiled=True
    )
    return lax.psum_scatter(
        jnp.dot(set_attended, w_out, preferred_element_type=jnp.float32, precision=highest),
        "col",
        scatter_dimension=0,
        tiled=True,
    )


def solution(mesh):
    depth, row, col = (mesh.shape[a] for a in ("depth", "row", "col"))
    split = jax.sharding.Mesh(
        np.asarray(mesh.devices).reshape(depth, row // 2, 2, col), ("depth", "rz", "rc", "col")
    )
    rows = ("rz", "rc")
    placed = (
        P(("depth", "col"), rows),
        P(rows, "col"),
        P(rows, "col"),
        P(rows, "col"),
        P("col", rows),
    )
    return jax.shard_map(
        on_device, mesh=split, in_specs=placed, out_specs=P(("depth", "col"), rows), check_vma=False
    )
```

profile of v0, /device:TPU:22, one launch (start us, length us, event | category | flops | bytes accessed | tf_op | source)
XLA Modules:
  0.0 403.2 jit_solution(6591100262648857011)
XLA Ops:
  6.5 0.0 copy-start
  6.5 0.0 all-gather.6.cloned.1.call-start
  6.5 0.7 all-gather.6.cloned.1.call-update
  7.3 0.0 reduce-scatter.4.cloned.1.call-start
  7.3 54.5 %all-gather.6.cloned.1.call-done = f32[2048,512]{1,0:T(8,128)} async-done(((f32[512,512]{1,0:T(8,128)}), f32[2048,512]{1,0:T(8,128)}) %all-gather.6.cloned.1.call-update) | async-done | bytes 4194320 | tf_op jit(solution)/shard_map/all_gather | solution.py:58
  61.8 0.0 copy-start.2
  61.8 4.6 %fusion.14 = f32[2048,128]{0,1:T(8,128)S(1)} fusion(f32[2048,512]{1,0:T(8,128)} %all-gather.6.cloned.1.call-done, f32[512,128]{1,0:T(8,128)} %param.8), kind=kOutput, calls=%fused_computation.17 | convolution fusion | flops 805306368 | bytes 5505024 | tf_op jit(solution)/shard_map/dot_general | solution.py:63
  66.4 0.0 copy-done.2
  66.4 3.2 fusion.13
  69.6 0.0 copy-done
  69.6 7.4 %fusion.12 = f32[2048,1024]{0,1:T(8,128)S(1)} fusion(f32[2048,512]{1,0:T(8,128)S(1)} %copy-done.2, f32[512,1024]{1,0:T(8,128)S(1)} %copy-done), kind=kOutput, calls=%fused_computation.15 | convolution fusion | flops 6442450944 | bytes 14680064 | tf_op jit(solution)/shard_map/dot_general | solution.py:63
  77.0 6.8 %pad_maximum_fusion = f32[2048,1280]{0,1:T(8,128)} fusion(f32[2048,128]{0,1:T(8,128)S(1)} %fusion.14, f32[2048,128]{0,1:T(8,128)S(1)} %fusion.13, f32[2048,1024]{0,1:T(8,128)S(1)} %fusion.12), kind=kLoop, calls=%fused_computation | loop fusion | flops 5242880 | bytes 20971520 | tf_op jit(solution)/shard_map/concatenate | solution.py:65
  83.7 0.0 reduce-scatter.4.cloned.1.call-update
  83.8 0.0 reduce-scatter.6.cloned.1.call-start
  83.8 25.8 %reduce-scatter.4.cloned.1.call-done = f32[1024,1280]{0,1:T(8,128)} async-done(((f32[2048,1280]{0,1:T(8,128)}), f32[1024,1280]{0,1:T(8,128)}) %reduce-scatter.4.cloned.1.call-update) | async-done | bytes 5242896 | tf_op jit(solution)/shard_map/reduce_scatter | solution.py:66
  109.7 0.0 reduce-scatter.6.cloned.1.call-update
  109.7 0.0 all-gather.8.cloned.1.call-start
  109.7 69.0 %reduce-scatter.6.cloned.1.call-done = f32[128,1280]{0,1:T(8,128)} async-done(((f32[1024,1280]{0,1:T(8,128)}), f32[128,1280]{0,1:T(8,128)}) %reduce-scatter.6.cloned.1.call-update) | async-done | bytes 655376 | tf_op jit(solution)/shard_map/reduce_scatter | solution.py:67
  178.7 1.6 slice.16
  180.3 0.0 all-gather.8.cloned.1.call-update
  180.3 0.0 all-gather.10.cloned.1.call-start
  180.4 38.3 %all-gather.8.cloned.1.call-done = f32[1024,256]{0,1:T(8,128)} async-done(((f32[128,256]{0,1:T(8,128)}), f32[1024,256]{0,1:T(8,128)}) %all-gather.8.cloned.1.call-update) | async-done | bytes 1048592 | tf_op jit(solution)/shard_map/all_gather | solution.py:70
  218.7 0.0 all-gather.10.cloned.1.call-update
  218.7 0.0 all-gather.12.cloned.1.call-start
  218.8 1.1 slice.18
  219.9 15.6 %all-gather.10.cloned.1.call-done = f32[2048,256]{0,1:T(8,128)} async-done(((f32[1024,256]{0,1:T(8,128)}), f32[2048,256]{0,1:T(8,128)}) %all-gather.10.cloned.1.call-update) | async-done | bytes 2097168 | tf_op jit(solution)/shard_map/all_gather | solution.py:70
  235.5 0.0 copy-start.3
  235.5 5.3 %bitcast_reduce_fusion = (f32[8,128]{1,0:T(8,128)S(1)}, f32[2048,128,8]{1,0,2:T(8,128)S(1)}) fusion(f32[128,8,128]{0,2,1:T(8,128)S(1)} %bitcast.44, f32[2048,256]{0,1:T(8,128)} %all-gather.10.cloned.1.call-done), kind=kOutput, calls=%fused_computation.4 | convolution fusion | flops 1614806016 | bytes 9965568 | tf_op jit(solution)/shard_map/rkgd,nkd->kgrn/dot_general | solution.py:37
  240.8 1.4 fusion.3
  242.2 0.0 copy-done.3
  242.2 4.2 %fusion.8 = f32[8,128,128]{1,2,0:T(8,128)} fusion(f32[2048,256]{0,1:T(8,128)S(1)} %copy-done.3, f32[2048,128,8]{1,0,2:T(8,128)S(1)} %get-tuple-element.6, f32[8,128]{1,0:T(8,128)S(1)} %broadcast_maximum_fusion, f32[8,128]{1,0:T(8,128)S(1)} %fusion.3), kind=kOutput, calls=%fused_computation.12 | convolution fusion | flops 1614938112 | bytes 9969664 | tf_op jit(solution)/shard_map/kgrn,nkd->kgrd/dot_general | solution.py:43
  246.4 0.0 all-gather.12.cloned.1.call-update
  246.4 0.0 all-gather.14.cloned.1.call-start
  246.4 63.7 %all-gather.12.cloned.1.call-done = f32[1024,1024]{0,1:T(8,128)} async-done(((f32[128,1024]{0,1:T(8,128)}), f32[1024,1024]{0,1:T(8,128)}) %all-gather.12.cloned.1.call-update) | async-done | bytes 4194320 | tf_op jit(solution)/shard_map/all_gather | solution.py:78
  310.1 0.0 all-gather.14.cloned.1.call-update
  310.2 0.0 copy-start.1
  310.2 0.0 reduce-scatter.8.cloned.1.call-start
  310.2 25.7 %all-gather.14.cloned.1.call-done = f32[2048,1024]{0,1:T(8,128)} async-done(((f32[1024,1024]{0,1:T(8,128)}), f32[2048,1024]{0,1:T(8,128)}) %all-gather.14.cloned.1.call-update) | async-done | bytes 8388624 | tf_op jit(solution)/shard_map/all_gather | solution.py:77
  335.9 11.1 %fusion.15 = f32[2048,512]{1,0:T(8,128)} fusion(f32[2048,1024]{0,1:T(8,128)} %all-gather.14.cloned.1.call-done, f32[1024,512]{1,0:T(8,128)} %param.9), kind=kOutput, calls=%fused_computation.18 | convolution fusion | flops 6442450944 | bytes 14680064 | tf_op jit(solution)/shard_map/dot_general | solution.py:81
  347.0 0.0 reduce-scatter.8.cloned.1.call-update
  347.0 49.3 %reduce-scatter.8.cloned.1.call-done = f32[512,512]{1,0:T(8,128)} async-done(((f32[2048,512]{1,0:T(8,128)}), f32[512,512]{1,0:T(8,128)}) %reduce-scatter.8.cloned.1.call-update) | async-done | bytes 1048592 | tf_op jit(solution)/shard_map/reduce_scatter | solution.py:80
  396.3 0.0 copy-done.1
  (1 shorter events, 0.0 us)
Async XLA Ops:
  6.5 63.0 %copy-start = (f32[512,1024]{1,0:T(8,128)S(1)}, f32[512,1024]{1,0:T(8,128)}, u32[]{:S(2)}) copy-start(f32[512,1024]{1,0:T(8,128)} %param.6) | copy-start | bytes 6291460
  6.5 55.3 %all-gather.6.cloned.1.call-start = ((), (), s32[]{:S(2)}) async-start(), calls=%async_computation.3 | async-start | bytes 5242880 | tf_op jit(solution)/shard_map/all_gather | solution.py:58
  7.3 102.4 %reduce-scatter.4.cloned.1.call-start = ((), (), s32[]{:S(2)}) async-start(), calls=%async_computation.4 | async-start | bytes 15728640 | tf_op jit(solution)/shard_map/reduce_scatter | solution.py:66
  61.8 4.6 %copy-start.2 = (f32[2048,512]{1,0:T(8,128)S(1)}, f32[2048,512]{1,0:T(8,128)}, u32[]{:S(2)}) copy-start(f32[2048,512]{1,0:T(8,128)} %all-gather.6.cloned.1.call-done) | copy-start | bytes 12582916
  83.8 95.0 %reduce-scatter.6.cloned.1.call-start = ((), (), s32[]{:S(2)}) async-start(), calls=%async_computation.5 | async-start | bytes 5898240 | tf_op jit(solution)/shard_map/reduce_scatter | solution.py:67
  109.7 109.0 %all-gather.8.cloned.1.call-start = ((), (), s32[]{:S(2)}) async-start(), calls=%async_computation.6 | async-start | bytes 1179648 | tf_op jit(solution)/shard_map/all_gather | solution.py:70
  180.3 55.1 %all-gather.10.cloned.1.call-start = ((), (), s32[]{:S(2)}) async-start(), calls=%async_computation.7 | async-start | bytes 3145728 | tf_op jit(solution)/shard_map/all_gather | solution.py:70
  218.7 91.4 %all-gather.12.cloned.1.call-start = ((), (), s32[]{:S(2)}) async-start(), calls=%async_computation.8 | async-start | bytes 4718592 | tf_op jit(solution)/shard_map/all_gather | solution.py:78
  235.5 6.7 %copy-start.3 = (f32[2048,256]{0,1:T(8,128)S(1)}, f32[2048,256]{0,1:T(8,128)}, u32[]{:S(2)}) copy-start(f32[2048,256]{0,1:T(8,128)} %all-gather.10.cloned.1.call-done) | copy-start | bytes 6291460
  246.4 89.5 %all-gather.14.cloned.1.call-start = ((), (), s32[]{:S(2)}) async-start(), calls=%async_computation.9 | async-start | bytes 12582912 | tf_op jit(solution)/shard_map/all_gather | solution.py:77
  310.2 86.2 %copy-start.1 = (f32[512,1024]{1,0:T(8,128)S(1)}, f32[512,1024]{1,0:T(8,128)}, u32[]{:S(2)}) copy-start(f32[512,1024]{1,0:T(8,128)} %param.6) | copy-start | bytes 6291460
  310.2 86.1 %reduce-scatter.8.cloned.1.call-start = ((), (), s32[]{:S(2)}) async-start(), calls=%async_computation.10 | async-start | bytes 5242880 | tf_op jit(solution)/shard_map/reduce_scatter | solution.py:80
Sparse Core Ops, SparseCore 0:
  9.2 52.6 all-gather.5
  83.9 25.7 reduce-scatter.3
  112.2 66.4 reduce-scatter.5
  180.5 38.1 all-gather.7
  220.3 15.0 all-gather.9
  246.5 63.5 all-gather.11
  311.9 23.9 all-gather.13
  347.1 49.1 reduce-scatter.7
where the time goes:
time: 406 us; the launch traced here: 403 us
  waiting for transfers between devices  343 us (84%)
  matrix products  35.7 us (9%)
  between operations  13.6 us (3%)
  other arithmetic  8.18 us (2%)
    reduce_scatter x1, waiting for transfers between devices, on_device(): joined = lax.psum_scatter(on_chip, 'rz', scatter_dimension=0, tiled=True)  69 us
    all_gather x1, waiting for transfers between devices, on_device(): lax.all_gather(attention_output, 'rz', axis=0, tiled=True)  63.7 us
    all_gather x1, waiting for transfers between devices, on_device(): gathered = lax.all_gather(tokens, 'col', axis=0, tiled=True)  54.5 us
    reduce_scatter x1, waiting for transfers between devices, on_device(): lax.psum_scatter(jnp.dot(set_attended, w_out, preferred_element_type=jnp....  49.3 us
    all_gather x1, waiting for transfers between devices, on_device(): lax.all_gather(local_kv, 'rz', axis=0, tiled=True)  38.3 us
    reduce_scatter x1, waiting for transfers between devices, on_device(): on_chip = lax.psum_scatter(partial, 'rc', scatter_dimension=0, tiled=True)  25.8 us
    all_gather x1, waiting for transfers between devices, on_device(): lax.all_gather(lax.all_gather(attention_output, 'rz', axis=0, tiled=True)...  25.7 us
    all_gather x1, waiting for transfers between devices, on_device(): lax.all_gather(lax.all_gather(local_kv, 'rz', axis=0, tiled=True), 'rc',...  15.6 us
  transfers between devices with their start and end apart: 8, of which 8 were waited for; matrix products, arithmetic and copies ran while one was open for 0% of the time, Pallas kernels for 0%

commit v1 on v0

--- a/solution.py
+++ b/solution.py
@@ -1,9 +1,12 @@
+import functools
 import math
 
 import jax
 import numpy as np
 import jax.numpy as jnp
 from jax import lax
+from jax.experimental import pallas as pl
+from jax.experimental.pallas import tpu as pltpu
 from jax.sharding import PartitionSpec as P
 
 QUERY_HEADS = 32
@@ -53,7 +56,84 @@
     )
 
 
-def on_device(tokens, w_query, w_key, w_value, w_out):
+def gather_kernel(ring, n, x_ref, out_ref, local_sem, send_sems, recv_sems):
+    mesh_id = pl.DeviceIdType.MESH
+    d = lax.axis_index("depth")
+    z = lax.axis_index("rz")
+    c = lax.axis_index("rc")
+    y = lax.axis_index("col")
+    right = lax.rem(z + 1, ring)
+    left = lax.rem(z + ring - 1, ring)
+    sib = (d, z, 1 - c, y)
+
+    barrier = pltpu.get_barrier_semaphore()
+    for peer in ((d, left, c, y), (d, right, c, y), sib):
+        pl.semaphore_signal(barrier, inc=1, device_id=peer, device_id_type=mesh_id)
+    pl.semaphore_wait(barrier, 3)
+
+    def rows(zz, lo=0, size=n):
+        return pl.ds(pl.multiple_of((zz * 2 + c) * n + lo, 8), size)
+
+    def remote(src, dst_rows, peer, idx):
+        cp = pltpu.make_async_remote_copy(
+            src_ref=src,
+            dst_ref=out_ref.at[dst_rows],
+            send_sem=send_sems.at[idx],
+            recv_sem=recv_sems.at[idx],
+            device_id=peer,
+            device_id_type=mesh_id,
+        )
+        cp.start()
+        return cp
+
+    local = pltpu.make_async_copy(x_ref, out_ref.at[rows(z)], local_sem)
+    local.start()
+    sib_copies = [remote(x_ref, rows(z), sib, ring)]
+    half = ring // 2
+    for s in range(1, half + 1):
+        origin_r = lax.rem(z - (s - 1) + ring, ring)
+        origin_l = lax.rem(z + (s - 1), ring)
+        src_r = x_ref if s == 1 else out_ref.at[rows(origin_r)]
+        src_l = x_ref if s == 1 else out_ref.at[rows(origin_l)]
+        if s < half:
+            cr = remote(src_r, rows(origin_r), (d, right, c, y), 2 * (s - 1))
+            cl = remote(src_l, rows(origin_l), (d, left, c, y), 2 * (s - 1) + 1)
+            cr.wait()
+            cl.wait()
+            got_l = lax.rem(z - s + ring, ring)
+            got_r = lax.rem(z + s, ring)
+            sib_copies.append(remote(out_ref.at[rows(got_l)], rows(got_l), sib, ring + 2 * s - 1))
+            sib_copies.append(remote(out_ref.at[rows(got_r)], rows(got_r), sib, ring + 2 * s))
+        else:
+            h = n // 2
+            cr = remote(src_r.at[pl.ds(0, h)], rows(origin_r, 0, h), (d, right, c, y), 2 * (s - 1))
+            cl = remote(src_l.at[pl.ds(h, h)], rows(origin_l, h, h), (d, left, c, y), 2 * (s - 1) + 1)
+            cr.wait()
+            cl.wait()
+            opp = lax.rem(z + half, ring)
+            sib_copies.append(remote(out_ref.at[rows(opp)], rows(opp), sib, ring + 2 * s - 1))
+    local.wait()
+    for cp in sib_copies:
+        cp.wait()
+
+
+def ring_gather(block, ring, collective_id):
+    n, w = block.shape
+    return pl.pallas_call(
+        functools.partial(gather_kernel, ring, n),
+        out_shape=jax.ShapeDtypeStruct((2 * ring * n, w), block.dtype),
+        in_specs=[pl.BlockSpec(memory_space=pl.ANY)],
+        out_specs=pl.BlockSpec(memory_space=pl.ANY),
+        scratch_shapes=[
+            pltpu.SemaphoreType.DMA(()),
+            pltpu.SemaphoreType.DMA((2 * ring,)),
+            pltpu.SemaphoreType.DMA((2 * ring,)),
+        ],
+        compiler_params=pltpu.CompilerParams(collective_id=collective_id, has_side_effects=True),
+    )(block)
+
+
+def on_device(ring, tokens, w_query, w_key, w_value, w_out):
     highest = lax.Precision.HIGH
     gathered = lax.all_gather(tokens, "col", axis=0, tiled=True)
     q_width = w_query.shape[1]
@@ -63,20 +143,15 @@
         return jnp.dot(gathered, weight, preferred_element_type=jnp.float32, precision=highest)
 
     partial = jnp.concatenate([product(w_query), product(w_key), product(w_value)], axis=1)
-    on_chip = lax.psum_scatter(partial, "rc", scatter_dimension=0, tiled=True)
-    joined = lax.psum_scatter(on_chip, "rz", scatter_dimension=0, tiled=True)
+    joined = lax.psum_scatter(partial, ("rz", "rc"), scatter_dimension=0, tiled=True)
     query_rows = joined[:, :q_width]
-    local_kv = joined[:, q_width:]
-    all_kv = lax.all_gather(lax.all_gather(local_kv, "rz", axis=0, tiled=True), "rc", axis=0, tiled=True)
+    all_kv = ring_gather(joined[:, q_width:], ring, 0)
     state_end = fold_keys(
         query_rows,
         start_state(query_rows, kv_width),
         (all_kv[:, :kv_width], all_kv[:, kv_width:]),
     )
-    attention_output = finish(state_end)
-    set_attended = lax.all_gather(
-        lax.all_gather(attention_output, "rz", axis=0, tiled=True), "rc", axis=0, tiled=True
-    )
+    set_attended = ring_gather(finish(state_end), ring, 1)
     return lax.psum_scatter(
         jnp.dot(set_attended, w_out, preferred_element_type=jnp.float32, precision=highest),
         "col",
@@ -99,5 +174,9 @@
         P("col", rows),
     )
     return jax.shard_map(
-        on_device, mesh=split, in_specs=placed, out_specs=P(("depth", "col"), rows), check_vma=False
+        functools.partial(on_device, row // 2),
+        mesh=split,
+        in_specs=placed,
+        out_specs=P(("depth", "col"), rows),
+        check_vma=False,
     )

time: 406 us -> 311 us (0.77)
  waiting for transfers between devices: 343 us -> 178 us
  Pallas kernels: 0 us -> 73.2 us
    all_gather x4 -> x0, waiting for transfers between devices: 143 us -> none  [the longest x1 63.7 us: on_device(): lax.all_gather(attention_output, 'rz', axis=0, tiled=True)]
    pallas_call x0 -> x2, Pallas kernels: none -> 73.2 us  [ring_gather(): pl.pallas_call(functools.partial(gather_kernel, ring, n), out_shape=jax.S...]
    reduce_scatter x2 -> x1, waiting for transfers between devices: 94.8 us -> 75.8 us  [on_device(): lax.psum_scatter(partial, ('rz', 'rc'), scatter_dimension=0, tiled=True)]
  transfers between devices with their start and end apart: 8 -> 3, of which waited for: 8 -> 3; matrix products, arithmetic and copies ran while one was open for 0% -> 0% of each run, Pallas kernels for 0% -> 0%
where the time goes in v1:
time: 311 us; the launch traced here: 308 us
  waiting for transfers between devices  178 us (57%)
  Pallas kernels  73.2 us (24%)
  matrix products  33.8 us (11%)
  between operations  13.2 us (4%)
  other arithmetic  6.5 us (2%)
    reduce_scatter x1, waiting for transfers between devices, on_device(): lax.psum_scatter(partial, ('rz', 'rc'), scatter_dimension=0, tiled=True)  75.8 us
    pallas_call x2, Pallas kernels, ring_gather(): pl.pallas_call(functools.partial(gather_kernel, ring, n), out_shape=jax.S...  73.2 us
    all_gather x1, waiting for transfers between devices, on_device(): gathered = lax.all_gather(tokens, 'col', axis=0, tiled=True)  54.5 us
    reduce_scatter x1, waiting for transfers between devices, on_device(): lax.psum_scatter(jnp.dot(set_attended, w_out, preferred_element_type=jnp....  47.4 us
    dot_general x3, matrix products, product(): jnp.dot(gathered, weight, preferred_element_type=jnp.float32, precision=h...  13.7 us
    dot_general x1, matrix products, on_device(): jnp.dot(set_attended, w_out, preferred_element_type=jnp.float32, precisio...  11.3 us
  transfers between devices with their start and end apart: 3, of which 3 were waited for; matrix products, arithmetic and copies ran while one was open for 0% of the time, Pallas kernels for 0%

profile of v1, /device:TPU:22, one launch (start us, length us, event | category | flops | bytes accessed | tf_op | source)
XLA Modules:
  0.0 308.0 jit_solution(14789416967604452429)
XLA Ops:
  6.5 0.0 copy-start
  6.5 0.0 all-gather.2.cloned.1.call-start
  6.5 0.7 all-gather.2.cloned.1.call-update
  7.3 0.0 reduce-scatter.3.cloned.1.call-start
  7.3 54.5 %all-gather.2.cloned.1.call-done = f32[2048,512]{1,0:T(8,128)} async-done(((f32[512,512]{1,0:T(8,128)}), f32[2048,512]{1,0:T(8,128)}) %all-gather.2.cloned.1.call-update) | async-done | bytes 4194320 | tf_op jit(solution)/shard_map/all_gather | solution.py:138
  61.8 0.0 copy-start.1
  61.8 4.2 %fusion.22 = f32[2048,128]{1,0:T(8,128)S(1)} fusion(f32[2048,512]{1,0:T(8,128)} %all-gather.2.cloned.1.call-done, f32[512,128]{1,0:T(8,128)} %param.8), kind=kOutput, calls=%fused_computation.22 | convolution fusion | flops 805306368 | bytes 5505024 | tf_op jit(solution)/shard_map/dot_general | solution.py:143
  66.0 0.0 copy-done.1
  66.0 2.8 fusion.21
  68.8 0.0 copy-done
  68.8 6.8 %fusion.20 = f32[2048,1024]{1,0:T(8,128)S(1)} fusion(f32[2048,512]{1,0:T(8,128)S(1)} %copy-done.1, f32[512,1024]{1,0:T(8,128)S(1)} %copy-done), kind=kOutput, calls=%fused_computation.20 | convolution fusion | flops 6442450944 | bytes 14680064 | tf_op jit(solution)/shard_map/dot_general | solution.py:143
  75.6 5.1 %pad_maximum_fusion = f32[2048,1280]{1,0:T(8,128)} fusion(f32[2048,128]{1,0:T(8,128)S(1)} %fusion.22, f32[2048,128]{1,0:T(8,128)S(1)} %fusion.21, f32[2048,1024]{1,0:T(8,128)S(1)} %fusion.20), kind=kLoop, calls=%fused_computation | loop fusion | flops 5242880 | bytes 20971520 | tf_op jit(solution)/shard_map/concatenate | solution.py:145
  80.7 0.0 reduce-scatter.3.cloned.1.call-update
  80.7 0.2 reduce-scatter.5.cloned.1.call-start
  81.0 75.8 %reduce-scatter.3.cloned.1.call-done = f32[128,1280]{1,0:T(8,128)} async-done(((f32[2048,1280]{1,0:T(8,128)}), f32[128,1280]{1,0:T(8,128)}) %reduce-scatter.3.cloned.1.call-update) | async-done | bytes 655376 | tf_op jit(solution)/shard_map/reduce_scatter | solution.py:146
  156.7 1.6 slice.16.x_ref
  158.3 23.0 %shard_map.55 = f32[2048,256]{1,0:T(8,128)} custom-call(f32[128,256]{1,0:T(8,128)} %slice.16.x_ref), custom_call_target="tpu_custom_call" | custom-call | tf_op jit(solution)/shard_map/pallas_call | solution.py:122
  181.3 0.0 copy-start.2
  181.3 5.4 %bitcast_reduce_fusion = (f32[8,128]{1,0:T(8,128)S(1)}, f32[2048,128,8]{1,0,2:T(8,128)S(1)}) fusion(f32[2048,256]{1,0:T(8,128)} %shard_map.55, f32[128,1280]{1,0:T(8,128)} %reduce-scatter.3.cloned.1.call-done), kind=kOutput, calls=%fused_computation.4 | convolution fusion | flops 1614806016 | bytes 9965568 | tf_op jit(solution)/shard_map/rkgd,nkd->kgrn/dot_general | solution.py:40
  186.7 1.4 fusion.3
  188.1 0.0 copy-done.2
  188.1 3.5 %fusion.12 = f32[8,128,128]{1,2,0:T(8,128)S(1)} fusion(f32[2048,256]{1,0:T(8,128)S(1)} %copy-done.2, f32[2048,128,8]{1,0,2:T(8,128)S(1)} %get-tuple-element.6, f32[8,128]{1,0:T(8,128)S(1)} %broadcast_maximum_fusion, f32[8,128]{1,0:T(8,128)S(1)} %fusion.3), kind=kOutput, calls=%fused_computation.14 | convolution fusion | flops 1614938112 | bytes 9969664 | tf_op jit(solution)/shard_map/kgrn,nkd->kgrd/dot_general | solution.py:46
  191.5 1.0 copy.19.x_ref
  192.5 50.2 %shard_map.56 = f32[2048,1024]{1,0:T(8,128)} custom-call(f32[128,1024]{1,0:T(8,128)} %copy.19.x_ref), custom_call_target="tpu_custom_call" | custom-call | tf_op jit(solution)/shard_map/pallas_call | solution.py:122
  242.8 11.3 %fusion.23 = f32[2048,512]{1,0:T(8,128)} fusion(f32[2048,1024]{1,0:T(8,128)} %shard_map.56, f32[1024,512]{1,0:T(8,128)} %param.9), kind=kOutput, calls=%fused_computation.23 | convolution fusion | flops 6442450944 | bytes 14680064 | tf_op jit(solution)/shard_map/dot_general | solution.py:156
  254.1 0.0 reduce-scatter.5.cloned.1.call-update
  254.1 47.4 %reduce-scatter.5.cloned.1.call-done = f32[512,512]{1,0:T(8,128)} async-done(((f32[2048,512]{1,0:T(8,128)}), f32[512,512]{1,0:T(8,128)}) %reduce-scatter.5.cloned.1.call-update) | async-done | bytes 1048592 | tf_op jit(solution)/shard_map/reduce_scatter | solution.py:155
  (1 shorter events, 0.0 us)
Async XLA Ops:
  6.5 62.2 %copy-start = (f32[512,1024]{1,0:T(8,128)S(1)}, f32[512,1024]{1,0:T(8,128)}, u32[]{:S(2)}) copy-start(f32[512,1024]{1,0:T(8,128)} %param.6) | copy-start | bytes 6291460
  6.5 55.3 %all-gather.2.cloned.1.call-start = ((), (), s32[]{:S(2)}) async-start(), calls=%async_computation.2 | async-start | bytes 5242880 | tf_op jit(solution)/shard_map/all_gather | solution.py:138
  7.3 149.5 %reduce-scatter.3.cloned.1.call-start = ((), (), s32[]{:S(2)}) async-start(), calls=%async_computation.3 | async-start | bytes 11141120 | tf_op jit(solution)/shard_map/reduce_scatter | solution.py:146
  61.8 4.2 %copy-start.1 = (f32[2048,512]{1,0:T(8,128)S(1)}, f32[2048,512]{1,0:T(8,128)}, u32[]{:S(2)}) copy-start(f32[2048,512]{1,0:T(8,128)} %all-gather.2.cloned.1.call-done) | copy-start | bytes 12582916
  80.7 220.8 %reduce-scatter.5.cloned.1.call-start = ((), (), s32[]{:S(2)}) async-start(), calls=%async_computation.4 | async-start | bytes 5242880 | tf_op jit(solution)/shard_map/reduce_scatter | solution.py:155
  181.3 6.8 %copy-start.2 = (f32[2048,256]{1,0:T(8,128)S(1)}, f32[2048,256]{1,0:T(8,128)}, u32[]{:S(2)}) copy-start(f32[2048,256]{1,0:T(8,128)} %shard_map.55) | copy-start | bytes 6291460
Sparse Core Ops, SparseCore 0:
  9.2 52.6 all-gather.1
  80.8 75.8 reduce-scatter.2
  254.2 47.2 reduce-scatter.4

commit v2 on v1

--- a/solution.py
+++ b/solution.py
@@ -56,23 +56,28 @@
     )
 
 
-def gather_kernel(ring, n, x_ref, out_ref, local_sem, send_sems, recv_sems):
+def gather_kernel(axis, ring, n, with_sib, x_ref, out_ref, local_sem, send_sems, recv_sems):
     mesh_id = pl.DeviceIdType.MESH
-    d = lax.axis_index("depth")
-    z = lax.axis_index("rz")
-    c = lax.axis_index("rc")
-    y = lax.axis_index("col")
-    right = lax.rem(z + 1, ring)
-    left = lax.rem(z + ring - 1, ring)
-    sib = (d, z, 1 - c, y)
+    names = ("depth", "rz", "rc", "col")
+    me = {a: lax.axis_index(a) for a in names}
+    pos = me[axis]
+
+    def device(**moved):
+        return tuple(moved.get(a, me[a]) for a in names)
+
+    right = device(**{axis: lax.rem(pos + 1, ring)})
+    left = device(**{axis: lax.rem(pos + ring - 1, ring)})
+    sib = device(rc=1 - me["rc"])
+    peers = (left, right, sib) if with_sib else (left, right)
 
     barrier = pltpu.get_barrier_semaphore()
-    for peer in ((d, left, c, y), (d, right, c, y), sib):
+    for peer in peers:
         pl.semaphore_signal(barrier, inc=1, device_id=peer, device_id_type=mesh_id)
-    pl.semaphore_wait(barrier, 3)
+    pl.semaphore_wait(barrier, len(peers))
 
-    def rows(zz, lo=0, size=n):
-        return pl.ds(pl.multiple_of((zz * 2 + c) * n + lo, 8), size)
+    def rows(at, lo=0, size=n):
+        slot = at * 2 + me["rc"] if with_sib else at
+        return pl.ds(pl.multiple_of(slot * n + lo, 8), size)
 
     def remote(src, dst_rows, peer, idx):
         cp = pltpu.make_async_remote_copy(
@@ -86,42 +91,44 @@
         cp.start()
         return cp
 
-    local = pltpu.make_async_copy(x_ref, out_ref.at[rows(z)], local_sem)
+    def to_sib(at, idx):
+        if with_sib:
+            sib_copies.append(remote(out_ref.at[rows(at)], rows(at), sib, idx))
+
+    local = pltpu.make_async_copy(x_ref, out_ref.at[rows(pos)], local_sem)
     local.start()
-    sib_copies = [remote(x_ref, rows(z), sib, ring)]
+    sib_copies = [remote(x_ref, rows(pos), sib, ring)] if with_sib else []
     half = ring // 2
     for s in range(1, half + 1):
-        origin_r = lax.rem(z - (s - 1) + ring, ring)
-        origin_l = lax.rem(z + (s - 1), ring)
+        origin_r = lax.rem(pos - (s - 1) + ring, ring)
+        origin_l = lax.rem(pos + (s - 1), ring)
         src_r = x_ref if s == 1 else out_ref.at[rows(origin_r)]
         src_l = x_ref if s == 1 else out_ref.at[rows(origin_l)]
         if s < half:
-            cr = remote(src_r, rows(origin_r), (d, right, c, y), 2 * (s - 1))
-            cl = remote(src_l, rows(origin_l), (d, left, c, y), 2 * (s - 1) + 1)
+            cr = remote(src_r, rows(origin_r), right, 2 * (s - 1))
+            cl = remote(src_l, rows(origin_l), left, 2 * (s - 1) + 1)
             cr.wait()
             cl.wait()
-            got_l = lax.rem(z - s + ring, ring)
-            got_r = lax.rem(z + s, ring)
-            sib_copies.append(remote(out_ref.at[rows(got_l)], rows(got_l), sib, ring + 2 * s - 1))
-            sib_copies.append(remote(out_ref.at[rows(got_r)], rows(got_r), sib, ring + 2 * s))
+            to_sib(lax.rem(pos - s + ring, ring), ring + 2 * s - 1)
+            to_sib(lax.rem(pos + s, ring), ring + 2 * s)
         else:
             h = n // 2
-            cr = remote(src_r.at[pl.ds(0, h)], rows(origin_r, 0, h), (d, right, c, y), 2 * (s - 1))
-            cl = remote(src_l.at[pl.ds(h, h)], rows(origin_l, h, h), (d, left, c, y), 2 * (s - 1) + 1)
+            cr = remote(src_r.at[pl.ds(0, h)], rows(origin_r, 0, h), right, 2 * (s - 1))
+            cl = remote(src_l.at[pl.ds(h, h)], rows(origin_l, h, h), left, 2 * (s - 1) + 1)
             cr.wait()
             cl.wait()
-            opp = lax.rem(z + half, ring)
-            sib_copies.append(remote(out_ref.at[rows(opp)], rows(opp), sib, ring + 2 * s - 1))
+            to_sib(lax.rem(pos + half, ring), ring + 2 * s - 1)
     local.wait()
     for cp in sib_copies:
         cp.wait()
 
 
-def ring_gather(block, ring, collective_id):
+def ring_gather(block, axis, ring, with_sib, collective_id):
     n, w = block.shape
+    copies = 2 if with_sib else 1
     return pl.pallas_call(
-        functools.partial(gather_kernel, ring, n),
-        out_shape=jax.ShapeDtypeStruct((2 * ring * n, w), block.dtype),
+        functools.partial(gather_kernel, axis, ring, n, with_sib),
+        out_shape=jax.ShapeDtypeStruct((copies * ring * n, w), block.dtype),
         in_specs=[pl.BlockSpec(memory_space=pl.ANY)],
         out_specs=pl.BlockSpec(memory_space=pl.ANY),
         scratch_shapes=[
@@ -133,9 +140,9 @@
     )(block)
 
 
-def on_device(ring, tokens, w_query, w_key, w_value, w_out):
+def on_device(ring, cols, tokens, w_query, w_key, w_value, w_out):
     highest = lax.Precision.HIGH
-    gathered = lax.all_gather(tokens, "col", axis=0, tiled=True)
+    gathered = ring_gather(tokens, "col", cols, False, 2)
     q_width = w_query.shape[1]
     kv_width = w_key.shape[1]
 
@@ -145,13 +152,13 @@
     partial = jnp.concatenate([product(w_query), product(w_key), product(w_value)], axis=1)
     joined = lax.psum_scatter(partial, ("rz", "rc"), scatter_dimension=0, tiled=True)
     query_rows = joined[:, :q_width]
-    all_kv = ring_gather(joined[:, q_width:], ring, 0)
+    all_kv = ring_gather(joined[:, q_width:], "rz", ring, True, 0)
     state_end = fold_keys(
         query_rows,
         start_state(query_rows, kv_width),
         (all_kv[:, :kv_width], all_kv[:, kv_width:]),
     )
-    set_attended = ring_gather(finish(state_end), ring, 1)
+    set_attended = ring_gather(finish(state_end), "rz", ring, True, 1)
     return lax.psum_scatter(
         jnp.dot(set_attended, w_out, preferred_element_type=jnp.float32, precision=highest),
         "col",
@@ -174,7 +181,7 @@
         P("col", rows),
     )
     return jax.shard_map(
-        functools.partial(on_device, row // 2),
+        functools.partial(on_device, row // 2, col),
         mesh=split,
         in_specs=placed,
         out_specs=P(("depth", "col"), rows),

time: 311 us -> 298 us (0.958)
  waiting for transfers between devices: 178 us -> 125 us
  Pallas kernels: 73.2 us -> 112 us
    all_gather x1 -> x0, waiting for transfers between devices: 54.5 us -> none  [on_device(): gathered = lax.all_gather(tokens, 'col', axis=0, tiled=True)]
    pallas_call x2 -> x3, Pallas kernels: 73.2 us -> 112 us  [ring_gather(): pl.pallas_call(functools.partial(gather_kernel, axis, ring, n, with_sib),...]
  transfers between devices with their start and end apart: 3 -> 2, of which waited for: 3 -> 2; matrix products, arithmetic and copies ran while one was open for 0% -> 0% of each run, Pallas kernels for 0% -> 0%
where the time goes in v2:
time: 298 us; the launch traced here: 295 us
  waiting for transfers between devices  125 us (42%)
  Pallas kernels  112 us (38%)
  matrix products  35 us (12%)
  between operations  13.5 us (5%)
  other arithmetic  6.51 us (2%)
    pallas_call x3, Pallas kernels, ring_gather(): pl.pallas_call(functools.partial(gather_kernel, axis, ring, n, with_sib),...  112 us
    reduce_scatter x1, waiting for transfers between devices, on_device(): lax.psum_scatter(partial, ('rz', 'rc'), scatter_dimension=0, tiled=True)  77.1 us
    reduce_scatter x1, waiting for transfers between devices, on_device(): lax.psum_scatter(jnp.dot(set_attended, w_out, preferred_element_type=jnp....  47.7 us
    dot_general x3, matrix products, product(): jnp.dot(gathered, weight, preferred_element_type=jnp.float32, precision=h...  14.9 us
    dot_general x1, matrix products, on_device(): jnp.dot(set_attended, w_out, preferred_element_type=jnp.float32, precisio...  11.3 us
  transfers between devices with their start and end apart: 2, of which 2 were waited for; matrix products, arithmetic and copies ran while one was open for 0% of the time, Pallas kernels for 0%

profile of v2, /device:TPU:22, one launch (start us, length us, event | category | flops | bytes accessed | tf_op | source)
XLA Modules:
  0.0 295.2 jit_solution(727822370410101474)
XLA Ops:
  6.5 0.0 copy-start
  6.5 0.0 copy-start.3
  6.5 0.0 reduce-scatter.3.cloned.1.call-start
  6.5 39.3 %shard_map.55 = f32[2048,512]{1,0:T(8,128)} custom-call(f32[512,512]{1,0:T(8,128)} %x_ref.1), custom_call_target="tpu_custom_call" | custom-call | tf_op jit(solution)/shard_map/pallas_call | solution.py:129
  45.8 0.0 copy-start.1
  45.8 4.2 %fusion.22 = f32[2048,128]{1,0:T(8,128)S(1)} fusion(f32[2048,512]{1,0:T(8,128)} %shard_map.55, f32[512,128]{1,0:T(8,128)} %param.8), kind=kOutput, calls=%fused_computation.22 | convolution fusion | flops 805306368 | bytes 5505024 | tf_op jit(solution)/shard_map/dot_general | solution.py:150
  50.0 0.0 copy-done.3
  50.0 4.0 %fusion.21 = f32[2048,128]{1,0:T(8,128)S(1)} fusion(f32[2048,512]{1,0:T(8,128)} %shard_map.55, f32[512,128]{1,0:T(8,128)S(1)} %copy-done.3), kind=kOutput, calls=%fused_computation.21 | convolution fusion | flops 805306368 | bytes 5505024 | tf_op jit(solution)/shard_map/dot_general | solution.py:150
  54.0 0.0 copy-done
  54.0 0.0 copy-done.1
  54.0 6.8 %fusion.20 = f32[2048,1024]{1,0:T(8,128)S(1)} fusion(f32[2048,512]{1,0:T(8,128)S(1)} %copy-done.1, f32[512,1024]{1,0:T(8,128)S(1)} %copy-done), kind=kOutput, calls=%fused_computation.20 | convolution fusion | flops 6442450944 | bytes 14680064 | tf_op jit(solution)/shard_map/dot_general | solution.py:150
  60.8 5.1 %pad_maximum_fusion = f32[2048,1280]{1,0:T(8,128)} fusion(f32[2048,128]{1,0:T(8,128)S(1)} %fusion.22, f32[2048,128]{1,0:T(8,128)S(1)} %fusion.21, f32[2048,1024]{1,0:T(8,128)S(1)} %fusion.20), kind=kLoop, calls=%fused_computation | loop fusion | flops 5242880 | bytes 20971520 | tf_op jit(solution)/shard_map/concatenate | solution.py:152
  65.9 0.0 reduce-scatter.3.cloned.1.call-update
  66.0 0.2 reduce-scatter.5.cloned.1.call-start
  66.2 77.1 %reduce-scatter.3.cloned.1.call-done = f32[128,1280]{1,0:T(8,128)} async-done(((f32[2048,1280]{1,0:T(8,128)}), f32[128,1280]{1,0:T(8,128)}) %reduce-scatter.3.cloned.1.call-update) | async-done | bytes 655376 | tf_op jit(solution)/shard_map/reduce_scatter | solution.py:153
  143.3 1.6 slice.16.x_ref
  144.9 22.9 %shard_map.56 = f32[2048,256]{1,0:T(8,128)} custom-call(f32[128,256]{1,0:T(8,128)} %slice.16.x_ref), custom_call_target="tpu_custom_call" | custom-call | tf_op jit(solution)/shard_map/pallas_call | solution.py:129
  167.8 0.0 copy-start.2
  167.8 5.4 %bitcast_reduce_fusion = (f32[8,128]{1,0:T(8,128)S(1)}, f32[2048,128,8]{1,0,2:T(8,128)S(1)}) fusion(f32[2048,256]{1,0:T(8,128)} %shard_map.56, f32[128,1280]{1,0:T(8,128)} %reduce-scatter.3.cloned.1.call-done), kind=kOutput, calls=%fused_computation.4 | convolution fusion | flops 1614806016 | bytes 9965568 | tf_op jit(solution)/shard_map/rkgd,nkd->kgrn/dot_general | solution.py:40
  173.2 1.4 fusion.3
  174.6 0.0 copy-done.2
  174.6 3.5 %fusion.12 = f32[8,128,128]{1,2,0:T(8,128)S(1)} fusion(f32[2048,256]{1,0:T(8,128)S(1)} %copy-done.2, f32[2048,128,8]{1,0,2:T(8,128)S(1)} %get-tuple-element.6, f32[8,128]{1,0:T(8,128)S(1)} %broadcast_maximum_fusion, f32[8,128]{1,0:T(8,128)S(1)} %fusion.3), kind=kOutput, calls=%fused_computation.14 | convolution fusion | flops 1614938112 | bytes 9969664 | tf_op jit(solution)/shard_map/kgrn,nkd->kgrd/dot_general | solution.py:46
  178.1 1.0 copy.19.x_ref
  179.1 50.3 %shard_map.57 = f32[2048,1024]{1,0:T(8,128)} custom-call(f32[128,1024]{1,0:T(8,128)} %copy.19.x_ref), custom_call_target="tpu_custom_call" | custom-call | tf_op jit(solution)/shard_map/pallas_call | solution.py:129
  229.3 11.3 %fusion.23 = f32[2048,512]{1,0:T(8,128)} fusion(f32[2048,1024]{1,0:T(8,128)} %shard_map.57, f32[1024,512]{1,0:T(8,128)} %param.9), kind=kOutput, calls=%fused_computation.23 | convolution fusion | flops 6442450944 | bytes 14680064 | tf_op jit(solution)/shard_map/dot_general | solution.py:163
  240.6 0.0 reduce-scatter.5.cloned.1.call-update
  240.6 47.7 %reduce-scatter.5.cloned.1.call-done = f32[512,512]{1,0:T(8,128)} async-done(((f32[2048,512]{1,0:T(8,128)}), f32[512,512]{1,0:T(8,128)}) %reduce-scatter.5.cloned.1.call-update) | async-done | bytes 1048592 | tf_op jit(solution)/shard_map/reduce_scatter | solution.py:162
  (1 shorter events, 0.0 us)
Async XLA Ops:
  6.5 47.5 %copy-start = (f32[512,1024]{1,0:T(8,128)S(1)}, f32[512,1024]{1,0:T(8,128)}, u32[]{:S(2)}) copy-start(f32[512,1024]{1,0:T(8,128)} %param.6) | copy-start | bytes 6291460
  6.5 43.5 %copy-start.3 = (f32[512,128]{1,0:T(8,128)S(1)}, f32[512,128]{1,0:T(8,128)}, u32[]{:S(2)}) copy-start(f32[512,128]{1,0:T(8,128)} %param.7) | copy-start | bytes 786436
  6.5 136.8 %reduce-scatter.3.cloned.1.call-start = ((), (), s32[]{:S(2)}) async-start(), calls=%async_computation.2 | async-start | bytes 11141120 | tf_op jit(solution)/shard_map/reduce_scatter | solution.py:153
  45.8 8.2 %copy-start.1 = (f32[2048,512]{1,0:T(8,128)S(1)}, f32[2048,512]{1,0:T(8,128)}, u32[]{:S(2)}) copy-start(f32[2048,512]{1,0:T(8,128)} %shard_map.55) | copy-start | bytes 12582916
  66.0 222.4 %reduce-scatter.5.cloned.1.call-start = ((), (), s32[]{:S(2)}) async-start(), calls=%async_computation.3 | async-start | bytes 5242880 | tf_op jit(solution)/shard_map/reduce_scatter | solution.py:162
  167.8 6.8 %copy-start.2 = (f32[2048,256]{1,0:T(8,128)S(1)}, f32[2048,256]{1,0:T(8,128)}, u32[]{:S(2)}) copy-start(f32[2048,256]{1,0:T(8,128)} %shard_map.56) | copy-start | bytes 6291460
Sparse Core Ops, SparseCore 0:
  66.1 77.1 reduce-scatter.2
  240.7 47.5 reduce-scatter.4

commit v3 on v2

--- a/solution.py
+++ b/solution.py
@@ -140,6 +140,109 @@
     )(block)
 
 
+def scatter_kernel(axis, ring, m, with_sib, x_ref, out_ref, sbuf, rbuf, sibbuf, send_sems, recv_sems, sib_sems):
+    mesh_id = pl.DeviceIdType.MESH
+    names = ("depth", "rz", "rc", "col")
+    me = {a: lax.axis_index(a) for a in names}
+    pos = me[axis]
+    h = m // 2
+
+    def device(**moved):
+        return tuple(moved.get(a, me[a]) for a in names)
+
+    right = device(**{axis: lax.rem(pos + 1, ring)})
+    left = device(**{axis: lax.rem(pos + ring - 1, ring)})
+    sib = device(rc=1 - me["rc"])
+    peers = (left, right, sib) if with_sib else (left, right)
+
+    barrier = pltpu.get_barrier_semaphore()
+    for peer in peers:
+        pl.semaphore_signal(barrier, inc=1, device_id=peer, device_id_type=mesh_id)
+    pl.semaphore_wait(barrier, len(peers))
+
+    def rows_of(at, half, owner):
+        slot = at * 2 + owner if with_sib else at
+        return pl.ds(pl.multiple_of(slot * m + half * h, 8), h)
+
+    def remote(src, dst, peer, sems, idx):
+        cp = pltpu.make_async_remote_copy(
+            src_ref=src,
+            dst_ref=dst,
+            send_sem=sems[0].at[idx],
+            recv_sem=sems[1].at[idx],
+            device_id=peer,
+            device_id_type=mesh_id,
+        )
+        cp.start()
+        return cp
+
+    def need(s, half):
+        sign = -1 if half == 0 else 1
+        return lax.rem(pos + sign * s + ring * ring, ring)
+
+    sib_copies = {}
+    if with_sib:
+        order = [(s, half) for s in range(1, ring) for half in (0, 1)] + [(ring, 0), (ring, 1)]
+        for idx, (s, half) in enumerate(order):
+            at = need(s % ring, half)
+            dst = sibbuf.at[pl.ds(pl.multiple_of(at * m + half * h, 8), h)]
+            sib_copies[(s, half)] = remote(
+                x_ref.at[rows_of(at, half, 1 - me["rc"])], dst, sib, (sib_sems[0], sib_sems[1]), idx
+            )
+
+    def contribution(s, half):
+        at = need(s % ring, half)
+        own = x_ref[rows_of(at, half, me["rc"])]
+        if with_sib:
+            sib_copies[(s, half)].wait()
+            own = own + sibbuf[pl.ds(pl.multiple_of(at * m + half * h, 8), h)]
+        return own
+
+    ring_copies = {}
+    for s in range(1, ring):
+        for half in (0, 1):
+            value = contribution(s, half)
+            if s > 1:
+                ring_copies[(s - 1, half)].wait()
+                value = value + rbuf[half, s - 2]
+            sbuf[half, s - 1] = value
+            ring_copies[(s, half)] = remote(
+                sbuf.at[half, s - 1],
+                rbuf.at[half, s - 1],
+                right if half == 0 else left,
+                (send_sems, recv_sems),
+                half * (ring - 1) + s - 1,
+            )
+    for half in (0, 1):
+        value = contribution(ring, half)
+        ring_copies[(ring - 1, half)].wait()
+        out_ref[pl.ds(half * h, h)] = value + rbuf[half, ring - 2]
+
+
+def ring_scatter(x, axis, ring, with_sib, collective_id):
+    total, w = x.shape
+    copies = 2 if with_sib else 1
+    m = total // (copies * ring)
+    sib_rows = ring * m if with_sib else 8
+    return pl.pallas_call(
+        functools.partial(scatter_kernel, axis, ring, m, with_sib),
+        out_shape=jax.ShapeDtypeStruct((m, w), x.dtype),
+        in_specs=[pl.BlockSpec(memory_space=pltpu.VMEM)],
+        out_specs=pl.BlockSpec(memory_space=pltpu.VMEM),
+        scratch_shapes=[
+            pltpu.VMEM((2, ring - 1, m // 2, w), x.dtype),
+            pltpu.VMEM((2, ring - 1, m // 2, w), x.dtype),
+            pltpu.VMEM((sib_rows, w), x.dtype),
+            pltpu.SemaphoreType.DMA((2 * ring,)),
+            pltpu.SemaphoreType.DMA((2 * ring,)),
+            (pltpu.SemaphoreType.DMA((2 * ring,)), pltpu.SemaphoreType.DMA((2 * ring,))),
+        ],
+        compiler_params=pltpu.CompilerParams(
+            collective_id=collective_id, has_side_effects=True, vmem_limit_bytes=60 * 1024 * 1024
+        ),
+    )(x)
+
+
 def on_device(ring, cols, tokens, w_query, w_key, w_value, w_out):
     highest = lax.Precision.HIGH
     gathered = ring_gather(tokens, "col", cols, False, 2)
@@ -150,7 +253,7 @@
         return jnp.dot(gathered, weight, preferred_element_type=jnp.float32, precision=highest)
 
     partial = jnp.concatenate([product(w_query), product(w_key), product(w_value)], axis=1)
-    joined = lax.psum_scatter(partial, ("rz", "rc"), scatter_dimension=0, tiled=True)
+    joined = ring_scatter(partial, "rz", ring, True, 3)
     query_rows = joined[:, :q_width]
     all_kv = ring_gather(joined[:, q_width:], "rz", ring, True, 0)
     state_end = fold_keys(
@@ -159,11 +262,12 @@
         (all_kv[:, :kv_width], all_kv[:, kv_width:]),
     )
     set_attended = ring_gather(finish(state_end), "rz", ring, True, 1)
-    return lax.psum_scatter(
+    return ring_scatter(
         jnp.dot(set_attended, w_out, preferred_element_type=jnp.float32, precision=highest),
         "col",
-        scatter_dimension=0,
-        tiled=True,
+        cols,
+        False,
+        4,
     )
 
 

time: 298 us -> 275 us (0.923)
  waiting for transfers between devices: 125 us -> 0 us
  Pallas kernels: 112 us -> 227 us
  between operations: 13.5 us -> 0.14 us
    reduce_scatter x2 -> x0, waiting for transfers between devices: 125 us -> none  [the longest x1 77.1 us: on_device(): lax.psum_scatter(partial, ('rz', 'rc'), scatter_dimension=0, tiled=True)]
    pallas_call x0 -> x2, Pallas kernels: none -> 114 us  [ring_scatter(): pl.pallas_call(functools.partial(scatter_kernel, axis, ring, m, with_sib)...]
  transfers between devices with their start and end apart: 2 -> 0, of which waited for: 2 -> 0; matrix products, arithmetic and copies ran while one was open for 0% -> 0% of each run, Pallas kernels for 0% -> 0%
where the time goes in v3:
time: 275 us; the launch traced here: 274 us
  Pallas kernels  227 us (83%)
  matrix products  35 us (13%)
  other arithmetic  6.51 us (2%)
  local copies, waits for them, and re-layouts  4.84 us (2%)
    pallas_call x2, Pallas kernels, ring_scatter(): pl.pallas_call(functools.partial(scatter_kernel, axis, ring, m, with_sib)...  114 us
    pallas_call x3, Pallas kernels, ring_gather(): pl.pallas_call(functools.partial(gather_kernel, axis, ring, n, with_sib),...  113 us
    dot_general x3, matrix products, product(): jnp.dot(gathered, weight, preferred_element_type=jnp.float32, precision=h...  14.9 us
    dot_general x1, matrix products, on_device(): jnp.dot(set_attended, w_out, preferred_element_type=jnp.float32, precisio...  11.3 us

profile of v3, /device:TPU:22, one launch (start us, length us, event | category | flops | bytes accessed | tf_op | source)
XLA Modules:
  0.0 273.8 jit_solution(15125990404334075544)
XLA Ops:
  0.0 0.0 copy-start
  0.0 0.0 copy-start.3
  0.0 39.3 %shard_map.55 = f32[2048,512]{1,0:T(8,128)} custom-call(f32[512,512]{1,0:T(8,128)} %x_ref.1), custom_call_target="tpu_custom_call" | custom-call | tf_op jit(solution)/shard_map/pallas_call | solution.py:129
  39.3 0.0 copy-start.1
  39.3 4.2 %fusion.22 = f32[2048,128]{1,0:T(8,128)S(1)} fusion(f32[2048,512]{1,0:T(8,128)} %shard_map.55, f32[512,128]{1,0:T(8,128)} %param.8), kind=kOutput, calls=%fused_computation.22 | convolution fusion | flops 805306368 | bytes 5505024 | tf_op jit(solution)/shard_map/dot_general | solution.py:253
  43.5 0.0 copy-done.3
  43.5 4.0 %fusion.21 = f32[2048,128]{1,0:T(8,128)S(1)} fusion(f32[2048,512]{1,0:T(8,128)} %shard_map.55, f32[512,128]{1,0:T(8,128)S(1)} %copy-done.3), kind=kOutput, calls=%fused_computation.21 | convolution fusion | flops 805306368 | bytes 5505024 | tf_op jit(solution)/shard_map/dot_general | solution.py:253
  47.5 0.0 copy-done
  47.5 0.0 copy-done.1
  47.5 6.8 %fusion.20 = f32[2048,1024]{1,0:T(8,128)S(1)} fusion(f32[2048,512]{1,0:T(8,128)S(1)} %copy-done.1, f32[512,1024]{1,0:T(8,128)S(1)} %copy-done), kind=kOutput, calls=%fused_computation.20 | convolution fusion | flops 6442450944 | bytes 14680064 | tf_op jit(solution)/shard_map/dot_general | solution.py:253
  54.3 5.1 %pad_maximum_fusion.x_ref = f32[2048,1280]{1,0:T(8,128)} fusion(f32[2048,128]{1,0:T(8,128)S(1)} %fusion.22, f32[2048,128]{1,0:T(8,128)S(1)} %fusion.21, f32[2048,1024]{1,0:T(8,128)S(1)} %fusion.20), kind=kLoop, calls=%fused_computation | loop fusion | flops 5242880 | bytes 20971520 | tf_op jit(solution)/shard_map/concatenate | solution.py:255
  59.5 69.0 %shard_map.56 = f32[128,1280]{1,0:T(8,128)} custom-call(f32[2048,1280]{1,0:T(8,128)} %pad_maximum_fusion.x_ref), custom_call_target="tpu_custom_call" | custom-call | tf_op jit(solution)/shard_map/pallas_call | solution.py:227
  128.5 1.6 slice.12.x_ref
  130.1 22.0 %shard_map.57 = f32[2048,256]{1,0:T(8,128)} custom-call(f32[128,256]{1,0:T(8,128)} %slice.12.x_ref), custom_call_target="tpu_custom_call" | custom-call | tf_op jit(solution)/shard_map/pallas_call | solution.py:129
  152.1 0.0 copy-start.2
  152.1 5.4 %bitcast_reduce_fusion = (f32[8,128]{1,0:T(8,128)S(1)}, f32[2048,128,8]{1,0,2:T(8,128)S(1)}) fusion(f32[2048,256]{1,0:T(8,128)} %shard_map.57, f32[128,1280]{1,0:T(8,128)} %shard_map.56), kind=kOutput, calls=%fused_computation.4 | convolution fusion | flops 1614806016 | bytes 9965568 | tf_op jit(solution)/shard_map/rkgd,nkd->kgrn/dot_general | solution.py:40
  157.5 1.4 fusion.3
  158.8 0.0 copy-done.2
  158.8 3.5 %fusion.12 = f32[8,128,128]{1,2,0:T(8,128)S(1)} fusion(f32[2048,256]{1,0:T(8,128)S(1)} %copy-done.2, f32[2048,128,8]{1,0,2:T(8,128)S(1)} %get-tuple-element.6, f32[8,128]{1,0:T(8,128)S(1)} %broadcast_maximum_fusion, f32[8,128]{1,0:T(8,128)S(1)} %fusion.3), kind=kOutput, calls=%fused_computation.14 | convolution fusion | flops 1614938112 | bytes 9969664 | tf_op jit(solution)/shard_map/kgrn,nkd->kgrd/dot_general | solution.py:46
  162.3 1.0 copy.19.x_ref
  163.3 51.9 %shard_map.58 = f32[2048,1024]{1,0:T(8,128)} custom-call(f32[128,1024]{1,0:T(8,128)} %copy.19.x_ref), custom_call_target="tpu_custom_call" | custom-call | tf_op jit(solution)/shard_map/pallas_call | solution.py:129
  215.2 11.3 %fusion.23.x_ref = f32[2048,512]{1,0:T(8,128)} fusion(f32[2048,1024]{1,0:T(8,128)} %shard_map.58, f32[1024,512]{1,0:T(8,128)} %param.9), kind=kOutput, calls=%fused_computation.23 | convolution fusion | flops 6442450944 | bytes 14680064 | tf_op jit(solution)/shard_map/dot_general | solution.py:266
  226.5 45.0 %shard_map.59 = f32[512,512]{1,0:T(8,128)} custom-call(f32[2048,512]{1,0:T(8,128)} %fusion.23.x_ref), custom_call_target="tpu_custom_call" | custom-call | tf_op jit(solution)/shard_map/pallas_call | solution.py:227
  271.5 2.3 copy.28
  (1 shorter events, 0.0 us)
Async XLA Ops:
  0.0 47.5 %copy-start = (f32[512,1024]{1,0:T(8,128)S(1)}, f32[512,1024]{1,0:T(8,128)}, u32[]{:S(2)}) copy-start(f32[512,1024]{1,0:T(8,128)} %param.6) | copy-start | bytes 6291460
  0.0 43.5 %copy-start.3 = (f32[512,128]{1,0:T(8,128)S(1)}, f32[512,128]{1,0:T(8,128)}, u32[]{:S(2)}) copy-start(f32[512,128]{1,0:T(8,128)} %param.7) | copy-start | bytes 786436
  39.3 8.2 %copy-start.1 = (f32[2048,512]{1,0:T(8,128)S(1)}, f32[2048,512]{1,0:T(8,128)}, u32[]{:S(2)}) copy-start(f32[2048,512]{1,0:T(8,128)} %shard_map.55) | copy-start | bytes 12582916
  152.1 6.8 %copy-start.2 = (f32[2048,256]{1,0:T(8,128)S(1)}, f32[2048,256]{1,0:T(8,128)}, u32[]{:S(2)}) copy-start(f32[2048,256]{1,0:T(8,128)} %shard_map.57) | copy-start | bytes 6291460

commit v4 on v3

--- a/solution.py
+++ b/solution.py
@@ -140,12 +140,13 @@
     )(block)
 
 
-def scatter_kernel(axis, ring, m, with_sib, x_ref, out_ref, sbuf, rbuf, sibbuf, send_sems, recv_sems, sib_sems):
+def scatter_kernel(axis, ring, m, with_sib, parts, x_ref, out_ref, sbuf, rbuf, sibbuf, send_sems, recv_sems, sib_sems):
     mesh_id = pl.DeviceIdType.MESH
     names = ("depth", "rz", "rc", "col")
     me = {a: lax.axis_index(a) for a in names}
     pos = me[axis]
     h = m // 2
+    q = h // parts
 
     def device(**moved):
         return tuple(moved.get(a, me[a]) for a in names)
@@ -160,9 +161,12 @@
         pl.semaphore_signal(barrier, inc=1, device_id=peer, device_id_type=mesh_id)
     pl.semaphore_wait(barrier, len(peers))
 
-    def rows_of(at, half, owner):
+    def rows_of(at, half, part, owner):
         slot = at * 2 + owner if with_sib else at
-        return pl.ds(pl.multiple_of(slot * m + half * h, 8), h)
+        return pl.ds(pl.multiple_of(slot * m + half * h + part * q, 8), q)
+
+    def sib_rows(at, half, part):
+        return pl.ds(pl.multiple_of(at * m + half * h + part * q, 8), q)
 
     def remote(src, dst, peer, sems, idx):
         cp = pltpu.make_async_remote_copy(
@@ -178,63 +182,69 @@
 
     def need(s, half):
         sign = -1 if half == 0 else 1
-        return lax.rem(pos + sign * s + ring * ring, ring)
+        return lax.rem(pos + sign * (s % ring) + ring * ring, ring)
 
     sib_copies = {}
     if with_sib:
-        order = [(s, half) for s in range(1, ring) for half in (0, 1)] + [(ring, 0), (ring, 1)]
+        order = [(s, half) for s in range(1, ring + 1) for half in (0, 1)]
         for idx, (s, half) in enumerate(order):
-            at = need(s % ring, half)
-            dst = sibbuf.at[pl.ds(pl.multiple_of(at * m + half * h, 8), h)]
+            at = need(s, half)
             sib_copies[(s, half)] = remote(
-                x_ref.at[rows_of(at, half, 1 - me["rc"])], dst, sib, (sib_sems[0], sib_sems[1]), idx
+                x_ref.at[pl.ds(pl.multiple_of((at * 2 + 1 - me["rc"]) * m + half * h, 8), h)],
+                sibbuf.at[pl.ds(pl.multiple_of(at * m + half * h, 8), h)],
+                sib,
+                (sib_sems[0], sib_sems[1]),
+                idx,
             )
 
-    def contribution(s, half):
-        at = need(s % ring, half)
-        own = x_ref[rows_of(at, half, me["rc"])]
+    def contribution(s, half, part):
+        at = need(s, half)
+        own = x_ref[rows_of(at, half, part, me["rc"])]
         if with_sib:
-            sib_copies[(s, half)].wait()
-            own = own + sibbuf[pl.ds(pl.multiple_of(at * m + half * h, 8), h)]
+            if part == 0:
+                sib_copies[(s, half)].wait()
+            own = own + sibbuf[sib_rows(at, half, part)]
         return own
 
     ring_copies = {}
     for s in range(1, ring):
+        for part in range(parts):
+            for half in (0, 1):
+                value = contribution(s, half, part)
+                if s > 1:
+                    ring_copies[(s - 1, half, part)].wait()
+                    value = value + rbuf[half, s - 2, part]
+                sbuf[half, s - 1, part] = value
+                ring_copies[(s, half, part)] = remote(
+                    sbuf.at[half, s - 1, part],
+                    rbuf.at[half, s - 1, part],
+                    right if half == 0 else left,
+                    (send_sems, recv_sems),
+                    (half * (ring - 1) + s - 1) * parts + part,
+                )
+    for part in range(parts):
         for half in (0, 1):
-            value = contribution(s, half)
-            if s > 1:
-                ring_copies[(s - 1, half)].wait()
-                value = value + rbuf[half, s - 2]
-            sbuf[half, s - 1] = value
-            ring_copies[(s, half)] = remote(
-                sbuf.at[half, s - 1],
-                rbuf.at[half, s - 1],
-                right if half == 0 else left,
-                (send_sems, recv_sems),
-                half * (ring - 1) + s - 1,
-            )
-    for half in (0, 1):
-        value = contribution(ring, half)
-        ring_copies[(ring - 1, half)].wait()
-        out_ref[pl.ds(half * h, h)] = value + rbuf[half, ring - 2]
-
-
-def ring_scatter(x, axis, ring, with_sib, collective_id):
+            value = contribution(ring, half, part)
+            ring_copies[(ring - 1, half, part)].wait()
+            out_ref[pl.ds(half * h + part * q, q)] = value + rbuf[half, ring - 2, part]
+
+
+def ring_scatter(x, axis, ring, with_sib, parts, collective_id):
     total, w = x.shape
     copies = 2 if with_sib else 1
     m = total // (copies * ring)
     sib_rows = ring * m if with_sib else 8
     return pl.pallas_call(
-        functools.partial(scatter_kernel, axis, ring, m, with_sib),
+        functools.partial(scatter_kernel, axis, ring, m, with_sib, parts),
         out_shape=jax.ShapeDtypeStruct((m, w), x.dtype),
         in_specs=[pl.BlockSpec(memory_space=pltpu.VMEM)],
         out_specs=pl.BlockSpec(memory_space=pltpu.VMEM),
         scratch_shapes=[
-            pltpu.VMEM((2, ring - 1, m // 2, w), x.dtype),
-            pltpu.VMEM((2, ring - 1, m // 2, w), x.dtype),
+            pltpu.VMEM((2, ring - 1, parts, m // 2 // parts, w), x.dtype),
+            pltpu.VMEM((2, ring - 1, parts, m // 2 // parts, w), x.dtype),
             pltpu.VMEM((sib_rows, w), x.dtype),
-            pltpu.SemaphoreType.DMA((2 * ring,)),
-            pltpu.SemaphoreType.DMA((2 * ring,)),
+            pltpu.SemaphoreType.DMA((2 * ring * parts,)),
+            pltpu.SemaphoreType.DMA((2 * ring * parts,)),
             (pltpu.SemaphoreType.DMA((2 * ring,)), pltpu.SemaphoreType.DMA((2 * ring,))),
         ],
         compiler_params=pltpu.CompilerParams(
@@ -252,8 +262,8 @@
     def product(weight):
         return jnp.dot(gathered, weight, preferred_element_type=jnp.float32, precision=highest)
 
-    partial = jnp.concatenate([product(w_query), product(w_key), product(w_value)], axis=1)
-    joined = ring_scatter(partial, "rz", ring, True, 3)
+    partial = product(jnp.concatenate([w_query, w_key, w_value], axis=1))
+    joined = ring_scatter(partial, "rz", ring, True, 4, 3)
     query_rows = joined[:, :q_width]
     all_kv = ring_gather(joined[:, q_width:], "rz", ring, True, 0)
     state_end = fold_keys(
@@ -268,6 +278,7 @@
         cols,
         False,
         4,
+        4,
     )
 
 

time: 275 us -> 261 us (0.949)
  Pallas kernels: 227 us -> 220 us
  other arithmetic: 6.51 us -> 1.37 us
    pallas_call x2, Pallas kernels: 114 us -> 107 us  [ring_scatter(): pl.pallas_call(functools.partial(scatter_kernel, axis, ring, m, with_sib,...]
    concatenate x1 -> x0, other arithmetic: 5.14 us -> none  [on_device(): jnp.concatenate([product(w_query), product(w_key), product(w_value)], axi...]
    dot_general x3 -> x1, matrix products: 14.9 us -> 13.3 us  [product(): jnp.dot(gathered, weight, preferred_element_type=jnp.float32, precision=h...]
where the time goes in v4:
time: 261 us; the launch traced here: 259 us
  Pallas kernels  220 us (84%)
  matrix products  32.7 us (13%)
  local copies, waits for them, and re-layouts  4.84 us (2%)
    pallas_call x3, Pallas kernels, ring_gather(): pl.pallas_call(functools.partial(gather_kernel, axis, ring, n, with_sib),...  113 us
    pallas_call x2, Pallas kernels, ring_scatter(): pl.pallas_call(functools.partial(scatter_kernel, axis, ring, m, with_sib,...  107 us
    dot_general x1, matrix products, product(): jnp.dot(gathered, weight, preferred_element_type=jnp.float32, precision=h...  13.3 us
    dot_general x1, matrix products, on_device(): jnp.dot(set_attended, w_out, preferred_element_type=jnp.float32, precisio...  10.6 us
    dot_general x1, matrix products, fold_keys(): jnp.einsum('rkgd,nkd->kgrn', query_head_rows, key_head_rows, precision=hi...  5.37 us

profile of v4, /device:TPU:22, one launch (start us, length us, event | category | flops | bytes accessed | tf_op | source)
XLA Modules:
  0.0 258.9 jit_solution(3015149367623326104)
XLA Ops:
  0.0 0.0 copy-start
  0.0 39.3 %shard_map.55 = f32[2048,512]{1,0:T(8,128)} custom-call(f32[512,512]{1,0:T(8,128)} %x_ref.1), custom_call_target="tpu_custom_call" | custom-call | tf_op jit(solution)/shard_map/pallas_call | solution.py:129
  39.3 13.3 %convolution_bitcast_fusion.x_ref = f32[2048,1280]{1,0:T(8,128)} fusion(f32[2048,512]{1,0:T(8,128)} %shard_map.55, f32[512,128]{1,0:T(8,128)} %param.8, f32[512,128]{1,0:T(8,128)} %param.7, f32[512,1024]{1,0:T(8,128)} %param.6), kind=kOutput, calls=%fused_computation | convolution fusion | flops 8054374400 | bytes 17301504 | tf_op jit(solution)/shard_map/dot_general | solution.py:263
  52.6 64.8 %shard_map.56 = f32[128,1280]{1,0:T(8,128)} custom-call(f32[2048,1280]{1,0:T(8,128)} %convolution_bitcast_fusion.x_ref), custom_call_target="tpu_custom_call" | custom-call | tf_op jit(solution)/shard_map/pallas_call | solution.py:237
  117.4 1.6 slice.12.x_ref
  119.0 23.4 %shard_map.57 = f32[2048,256]{1,0:T(8,128)} custom-call(f32[128,256]{1,0:T(8,128)} %slice.12.x_ref), custom_call_target="tpu_custom_call" | custom-call | tf_op jit(solution)/shard_map/pallas_call | solution.py:129
  142.3 0.0 copy-start.1
  142.4 5.4 %bitcast_reduce_fusion = (f32[8,128]{1,0:T(8,128)S(1)}, f32[2048,128,8]{1,0,2:T(8,128)S(1)}) fusion(f32[2048,256]{1,0:T(8,128)} %shard_map.57, f32[128,1280]{1,0:T(8,128)} %shard_map.56), kind=kOutput, calls=%fused_computation.4 | convolution fusion | flops 1614806016 | bytes 9965568 | tf_op jit(solution)/shard_map/rkgd,nkd->kgrn/dot_general | solution.py:40
  147.7 1.4 fusion.3
  149.1 0.0 copy-done.1
  149.1 3.5 %fusion.17 = f32[8,128,128]{1,2,0:T(8,128)S(1)} fusion(f32[2048,256]{1,0:T(8,128)S(1)} %copy-done.1, f32[2048,128,8]{1,0,2:T(8,128)S(1)} %get-tuple-element.6, f32[8,128]{1,0:T(8,128)S(1)} %broadcast_maximum_fusion, f32[8,128]{1,0:T(8,128)S(1)} %fusion.3), kind=kOutput, calls=%fused_computation.19 | convolution fusion | flops 1614938112 | bytes 9969664 | tf_op jit(solution)/shard_map/kgrn,nkd->kgrd/dot_general | solution.py:46
  152.6 1.0 copy.15.x_ref
  153.6 50.6 %shard_map.58 = f32[2048,1024]{1,0:T(8,128)} custom-call(f32[128,1024]{1,0:T(8,128)} %copy.15.x_ref), custom_call_target="tpu_custom_call" | custom-call | tf_op jit(solution)/shard_map/pallas_call | solution.py:129
  204.2 0.0 copy-done
  204.2 10.6 %fusion.26.x_ref = f32[2048,512]{1,0:T(8,128)} fusion(f32[2048,1024]{1,0:T(8,128)} %shard_map.58, f32[1024,512]{1,0:T(8,128)S(1)} %copy-done), kind=kOutput, calls=%fused_computation.26 | convolution fusion | flops 6442450944 | bytes 14680064 | tf_op jit(solution)/shard_map/dot_general | solution.py:276
  214.8 41.8 %shard_map.59 = f32[512,512]{1,0:T(8,128)} custom-call(f32[2048,512]{1,0:T(8,128)} %fusion.26.x_ref), custom_call_target="tpu_custom_call" | custom-call | tf_op jit(solution)/shard_map/pallas_call | solution.py:237
  256.6 2.3 copy.24
  (1 shorter events, 0.0 us)
Async XLA Ops:
  0.0 204.2 %copy-start = (f32[1024,512]{1,0:T(8,128)S(1)}, f32[1024,512]{1,0:T(8,128)}, u32[]{:S(2)}) copy-start(f32[1024,512]{1,0:T(8,128)} %param.9) | copy-start | bytes 6291460
  142.3 6.8 %copy-start.1 = (f32[2048,256]{1,0:T(8,128)S(1)}, f32[2048,256]{1,0:T(8,128)}, u32[]{:S(2)}) copy-start(f32[2048,256]{1,0:T(8,128)} %shard_map.57) | copy-start | bytes 6291460

commit v5 on v4

--- a/solution.py
+++ b/solution.py
@@ -253,6 +253,134 @@
     )(x)
 
 
+def mix_kernel(ring, cols, n, o_ref, wo_ref, out_ref, ogath, part, recv, send_sems, recv_sems, y_send, y_recv):
+    mesh_id = pl.DeviceIdType.MESH
+    names = ("depth", "rz", "rc", "col")
+    me = {a: lax.axis_index(a) for a in names}
+    z, c, y = me["rz"], me["rc"], me["col"]
+    per_col = 2 * ring // cols
+
+    def device(**moved):
+        return tuple(moved.get(a, me[a]) for a in names)
+
+    right = device(rz=lax.rem(z + 1, ring))
+    left = device(rz=lax.rem(z + ring - 1, ring))
+    sib = device(rc=1 - c)
+    peers = [left, right, sib] + [device(col=lax.rem(y + d, cols)) for d in range(1, cols)]
+
+    barrier = pltpu.get_barrier_semaphore()
+    for peer in peers:
+        pl.semaphore_signal(barrier, inc=1, device_id=peer, device_id_type=mesh_id)
+    pl.semaphore_wait(barrier, len(peers))
+
+    def remote(src, dst, peer, send, recv_sem):
+        cp = pltpu.make_async_remote_copy(
+            src_ref=src, dst_ref=dst, send_sem=send, recv_sem=recv_sem, device_id=peer, device_id_type=mesh_id
+        )
+        cp.start()
+        return cp
+
+    def project(block, k):
+        part[k] = jnp.dot(block, wo_ref[...], preferred_element_type=jnp.float32, precision=lax.Precision.HIGH)
+        dest = k // per_col
+
+        @pl.when(dest != y)
+        def _():
+            remote(
+                part.at[k],
+                recv.at[lax.rem(y - dest + cols, cols), lax.rem(k, per_col)],
+                device(col=dest),
+                y_send.at[k],
+                y_recv.at[lax.rem(y - dest + cols, cols) * per_col + lax.rem(k, per_col)],
+            )
+
+    def slot(zz, cc):
+        return zz * 2 + cc
+
+    def z_copy(src, dst_slot, lo, size, peer, idx):
+        return remote(src, ogath.at[dst_slot, pl.ds(lo, size)], peer, send_sems.at[idx], recv_sems.at[idx])
+
+    project(o_ref[...], slot(z, c))
+    pending_sib = [(z_copy(o_ref, slot(z, c), 0, n, sib, ring), z)]
+    half = ring // 2
+    for s in range(1, half + 1):
+        origin_r = lax.rem(z - (s - 1) + ring, ring)
+        origin_l = lax.rem(z + (s - 1), ring)
+        src_r = o_ref if s == 1 else ogath.at[slot(origin_r, c)]
+        src_l = o_ref if s == 1 else ogath.at[slot(origin_l, c)]
+        if s < half:
+            cr = z_copy(src_r, slot(origin_r, c), 0, n, right, 2 * (s - 1))
+            cl = z_copy(src_l, slot(origin_l, c), 0, n, left, 2 * (s - 1) + 1)
+        else:
+            h = n // 2
+            cr = z_copy(src_r.at[pl.ds(0, h)], slot(origin_r, c), 0, h, right, 2 * (s - 1))
+            cl = z_copy(src_l.at[pl.ds(h, h)], slot(origin_l, c), h, h, left, 2 * (s - 1) + 1)
+        for cp, at in pending_sib:
+            cp.wait()
+            project(ogath[slot(at, 1 - c)], slot(at, 1 - c))
+        pending_sib = []
+        cr.wait()
+        cl.wait()
+        if s < half:
+            arrived = [(lax.rem(z - s + ring, ring), ring + 2 * s - 1), (lax.rem(z + s, ring), ring + 2 * s)]
+        else:
+            arrived = [(lax.rem(z + half, ring), ring + 2 * s - 1)]
+        for at, idx in arrived:
+            pending_sib.append((z_copy(ogath.at[slot(at, c)], slot(at, c), 0, n, sib, idx), at))
+            project(ogath[slot(at, c)], slot(at, c))
+    for cp, at in pending_sib:
+        cp.wait()
+        project(ogath[slot(at, 1 - c)], slot(at, 1 - c))
+    for i in range(per_col):
+        total = part[y * per_col + i]
+        for d in range(1, cols):
+            pltpu.make_async_remote_copy(
+                src_ref=part.at[0],
+                dst_ref=recv.at[d, i],
+                send_sem=y_send.at[0],
+                recv_sem=y_recv.at[d * per_col + i],
+                device_id=device(col=lax.rem(y + d, cols)),
+                device_id_type=mesh_id,
+            ).wait_recv()
+            total = total + recv[d, i]
+        out_ref[pl.ds(i * n, n)] = total
+    for k in range(2 * ring):
+        @pl.when(k // per_col != y)
+        def _():
+            pltpu.make_async_remote_copy(
+                src_ref=part.at[k],
+                dst_ref=recv.at[0, 0],
+                send_sem=y_send.at[k],
+                recv_sem=y_recv.at[0],
+                device_id=device(col=lax.rem(y + 1, cols)),
+                device_id_type=mesh_id,
+            ).wait_send()
+
+
+def gather_mix(o, w_out, ring, cols, collective_id):
+    n, width = o.shape
+    out_w = w_out.shape[1]
+    per_col = 2 * ring // cols
+    return pl.pallas_call(
+        functools.partial(mix_kernel, ring, cols, n),
+        out_shape=jax.ShapeDtypeStruct((per_col * n, out_w), jnp.float32),
+        in_specs=[pl.BlockSpec(memory_space=pltpu.VMEM), pl.BlockSpec(memory_space=pltpu.VMEM)],
+        out_specs=pl.BlockSpec(memory_space=pltpu.VMEM),
+        scratch_shapes=[
+            pltpu.VMEM((2 * ring, n, width), jnp.float32),
+            pltpu.VMEM((2 * ring, n, out_w), jnp.float32),
+            pltpu.VMEM((cols, per_col, n, out_w), jnp.float32),
+            pltpu.SemaphoreType.DMA((2 * ring,)),
+            pltpu.SemaphoreType.DMA((2 * ring,)),
+            pltpu.SemaphoreType.DMA((2 * ring,)),
+            pltpu.SemaphoreType.DMA((cols * per_col,)),
+        ],
+        compiler_params=pltpu.CompilerParams(
+            collective_id=collective_id, has_side_effects=True, vmem_limit_bytes=60 * 1024 * 1024
+        ),
+    )(o, w_out)
+
+
 def on_device(ring, cols, tokens, w_query, w_key, w_value, w_out):
     highest = lax.Precision.HIGH
     gathered = ring_gather(tokens, "col", cols, False, 2)
@@ -271,15 +399,7 @@
         start_state(query_rows, kv_width),
         (all_kv[:, :kv_width], all_kv[:, kv_width:]),
     )
-    set_attended = ring_gather(finish(state_end), "rz", ring, True, 1)
-    return ring_scatter(
-        jnp.dot(set_attended, w_out, preferred_element_type=jnp.float32, precision=highest),
-        "col",
-        cols,
-        False,
-        4,
-        4,
-    )
+    return gather_mix(finish(state_end), w_out, ring, cols, 5)
 
 
 def solution(mesh):

time: 261 us -> 250 us (0.958)
  matrix products: 32.7 us -> 22.1 us
    pallas_call x0 -> x1, Pallas kernels: none -> 93.5 us  [gather_mix(): pl.pallas_call(functools.partial(mix_kernel, ring, cols, n), out_shape=ja...]
    pallas_call x3 -> x2, Pallas kernels: 113 us -> 62.6 us  [ring_gather(): pl.pallas_call(functools.partial(gather_kernel, axis, ring, n, with_sib),...]
    pallas_call x2 -> x1, Pallas kernels: 107 us -> 64.8 us  [ring_scatter(): pl.pallas_call(functools.partial(scatter_kernel, axis, ring, m, with_sib,...]
    dot_general x1 -> x0, matrix products: 10.6 us -> none  [on_device(): jnp.dot(set_attended, w_out, preferred_element_type=jnp.float32, precisio...]
where the time goes in v5:
time: 250 us; the launch traced here: 249 us
  Pallas kernels  221 us (88%)
  matrix products  22.1 us (9%)
  local copies, waits for them, and re-layouts  4.83 us (2%)
    pallas_call x1, Pallas kernels, gather_mix(): pl.pallas_call(functools.partial(mix_kernel, ring, cols, n), out_shape=ja...  93.5 us
    pallas_call x1, Pallas kernels, ring_scatter(): pl.pallas_call(functools.partial(scatter_kernel, axis, ring, m, with_sib,...  64.8 us
    pallas_call x2, Pallas kernels, ring_gather(): pl.pallas_call(functools.partial(gather_kernel, axis, ring, n, with_sib),...  62.6 us
    dot_general x1, matrix products, product(): jnp.dot(gathered, weight, preferred_element_type=jnp.float32, precision=h...  13.3 us
    dot_general x1, matrix products, fold_keys(): jnp.einsum('rkgd,nkd->kgrn', query_head_rows, key_head_rows, precision=hi...  5.37 us

profile of v5, /device:TPU:22, one launch (start us, length us, event | category | flops | bytes accessed | tf_op | source)
XLA Modules:
  0.0 249.3 jit_solution(2483618635537761119)
XLA Ops:
  0.0 39.3 %shard_map.55 = f32[2048,512]{1,0:T(8,128)} custom-call(f32[512,512]{1,0:T(8,128)} %x_ref.1), custom_call_target="tpu_custom_call" | custom-call | tf_op jit(solution)/shard_map/pallas_call | solution.py:129
  39.3 13.3 %convolution_bitcast_fusion.x_ref = f32[2048,1280]{1,0:T(8,128)} fusion(f32[2048,512]{1,0:T(8,128)} %shard_map.55, f32[512,128]{1,0:T(8,128)} %param.8, f32[512,128]{1,0:T(8,128)} %param.7, f32[512,1024]{1,0:T(8,128)} %param.6), kind=kOutput, calls=%fused_computation | convolution fusion | flops 8054374400 | bytes 17301504 | tf_op jit(solution)/shard_map/dot_general | solution.py:391
  52.6 64.8 %shard_map.56 = f32[128,1280]{1,0:T(8,128)} custom-call(f32[2048,1280]{1,0:T(8,128)} %convolution_bitcast_fusion.x_ref), custom_call_target="tpu_custom_call" | custom-call | tf_op jit(solution)/shard_map/pallas_call | solution.py:237
  117.4 1.6 slice.12.x_ref
  119.0 23.4 %shard_map.57 = f32[2048,256]{1,0:T(8,128)} custom-call(f32[128,256]{1,0:T(8,128)} %slice.12.x_ref), custom_call_target="tpu_custom_call" | custom-call | tf_op jit(solution)/shard_map/pallas_call | solution.py:129
  142.3 0.0 copy-start
  142.4 5.4 %bitcast_reduce_fusion = (f32[8,128]{1,0:T(8,128)S(1)}, f32[2048,128,8]{1,0,2:T(8,128)S(1)}) fusion(f32[2048,256]{1,0:T(8,128)} %shard_map.57, f32[128,1280]{1,0:T(8,128)} %shard_map.56), kind=kOutput, calls=%fused_computation.4 | convolution fusion | flops 1614806016 | bytes 9965568 | tf_op jit(solution)/shard_map/rkgd,nkd->kgrn/dot_general | solution.py:40
  147.7 1.4 fusion.3
  149.1 0.0 copy-done
  149.1 3.5 %fusion.17 = f32[8,128,128]{1,2,0:T(8,128)S(1)} fusion(f32[2048,256]{1,0:T(8,128)S(1)} %copy-done, f32[2048,128,8]{1,0,2:T(8,128)S(1)} %get-tuple-element.6, f32[8,128]{1,0:T(8,128)S(1)} %broadcast_maximum_fusion, f32[8,128]{1,0:T(8,128)S(1)} %fusion.3), kind=kOutput, calls=%fused_computation.19 | convolution fusion | flops 1614938112 | bytes 9969664 | tf_op jit(solution)/shard_map/kgrn,nkd->kgrd/dot_general | solution.py:46
  152.6 1.0 copy.15.o_ref
  153.6 93.5 %shard_map.58 = f32[512,512]{1,0:T(8,128)} custom-call(f32[128,1024]{1,0:T(8,128)} %copy.15.o_ref, f32[1024,512]{1,0:T(8,128)} %wo_ref.1), custom_call_target="tpu_custom_call" | custom-call | tf_op jit(solution)/shard_map/pallas_call | solution.py:364
  247.1 2.3 copy.24
  (1 shorter events, 0.0 us)
Async XLA Ops:
  142.3 6.8 %copy-start = (f32[2048,256]{1,0:T(8,128)S(1)}, f32[2048,256]{1,0:T(8,128)}, u32[]{:S(2)}) copy-start(f32[2048,256]{1,0:T(8,128)} %shard_map.57) | copy-start | bytes 6291460

commit v6 on v5

--- a/solution.py
+++ b/solution.py
@@ -280,18 +280,18 @@
         cp.start()
         return cp
 
+    piece = n // cols
+
     def project(block, k):
         part[k] = jnp.dot(block, wo_ref[...], preferred_element_type=jnp.float32, precision=lax.Precision.HIGH)
-        dest = k // per_col
-
-        @pl.when(dest != y)
-        def _():
+        for d in range(1, cols):
+            dest = lax.rem(y + d, cols)
             remote(
-                part.at[k],
-                recv.at[lax.rem(y - dest + cols, cols), lax.rem(k, per_col)],
+                part.at[k, pl.ds(pl.multiple_of(dest * piece, 8), piece)],
+                recv.at[cols - d, k],
                 device(col=dest),
-                y_send.at[k],
-                y_recv.at[lax.rem(y - dest + cols, cols) * per_col + lax.rem(k, per_col)],
+                y_send.at[k * cols + d],
+                y_recv.at[(cols - d) * 2 * ring + k],
             )
 
     def slot(zz, cc):
@@ -331,28 +331,27 @@
     for cp, at in pending_sib:
         cp.wait()
         project(ogath[slot(at, 1 - c)], slot(at, 1 - c))
-    for i in range(per_col):
-        total = part[y * per_col + i]
+    for k in range(2 * ring):
+        total = part[k, pl.ds(pl.multiple_of(y * piece, 8), piece)]
         for d in range(1, cols):
             pltpu.make_async_remote_copy(
-                src_ref=part.at[0],
-                dst_ref=recv.at[d, i],
+                src_ref=part.at[k, pl.ds(0, piece)],
+                dst_ref=recv.at[d, k],
                 send_sem=y_send.at[0],
-                recv_sem=y_recv.at[d * per_col + i],
+                recv_sem=y_recv.at[d * 2 * ring + k],
                 device_id=device(col=lax.rem(y + d, cols)),
                 device_id_type=mesh_id,
             ).wait_recv()
-            total = total + recv[d, i]
-        out_ref[pl.ds(i * n, n)] = total
+            total = total + recv[d, k]
+        out_ref[pl.ds(k * piece, piece)] = total
     for k in range(2 * ring):
-        @pl.when(k // per_col != y)
-        def _():
+        for d in range(1, cols):
             pltpu.make_async_remote_copy(
-                src_ref=part.at[k],
+                src_ref=part.at[k, pl.ds(0, piece)],
                 dst_ref=recv.at[0, 0],
-                send_sem=y_send.at[k],
+                send_sem=y_send.at[k * cols + d],
                 recv_sem=y_recv.at[0],
-                device_id=device(col=lax.rem(y + 1, cols)),
+                device_id=device(col=lax.rem(y + d, cols)),
                 device_id_type=mesh_id,
             ).wait_send()
 
@@ -369,11 +368,11 @@
         scratch_shapes=[
             pltpu.VMEM((2 * ring, n, width), jnp.float32),
             pltpu.VMEM((2 * ring, n, out_w), jnp.float32),
-            pltpu.VMEM((cols, per_col, n, out_w), jnp.float32),
+            pltpu.VMEM((cols, 2 * ring, n // cols, out_w), jnp.float32),
             pltpu.SemaphoreType.DMA((2 * ring,)),
             pltpu.SemaphoreType.DMA((2 * ring,)),
-            pltpu.SemaphoreType.DMA((2 * ring,)),
-            pltpu.SemaphoreType.DMA((cols * per_col,)),
+            pltpu.SemaphoreType.DMA((2 * ring * cols,)),
+            pltpu.SemaphoreType.DMA((2 * ring * cols,)),
         ],
         compiler_params=pltpu.CompilerParams(
             collective_id=collective_id, has_side_effects=True, vmem_limit_bytes=60 * 1024 * 1024
@@ -381,17 +380,144 @@
     )(o, w_out)
 
 
+def front_kernel(ring, cols, tok_ref, w_ref, out_ref, tg, partial, sibbuf, sbuf, rbuf, y_sems, z_sems, sib_sems):
+    mesh_id = pl.DeviceIdType.MESH
+    names = ("depth", "rz", "rc", "col")
+    me = {a: lax.axis_index(a) for a in names}
+    z, c, y = me["rz"], me["rc"], me["col"]
+    rows = tok_ref.shape[0]
+    m = rows // (2 * ring)
+    h = m // 2
+
+    def device(**moved):
+        return tuple(moved.get(a, me[a]) for a in names)
+
+    right = device(rz=lax.rem(z + 1, ring))
+    left = device(rz=lax.rem(z + ring - 1, ring))
+    sib = device(rc=1 - c)
+    y_right = device(col=lax.rem(y + 1, cols))
+    y_left = device(col=lax.rem(y + cols - 1, cols))
+    peers = [left, right, sib, y_left, y_right]
+
+    barrier = pltpu.get_barrier_semaphore()
+    for peer in peers:
+        pl.semaphore_signal(barrier, inc=1, device_id=peer, device_id_type=mesh_id)
+    pl.semaphore_wait(barrier, len(peers))
+
+    def remote(src, dst, peer, sems, idx):
+        cp = pltpu.make_async_remote_copy(
+            src_ref=src, dst_ref=dst, send_sem=sems[0].at[idx], recv_sem=sems[1].at[idx],
+            device_id=peer, device_id_type=mesh_id,
+        )
+        cp.start()
+        return cp
+
+    def need(s, half):
+        sign = -1 if half == 0 else 1
+        return lax.rem(z + sign * (s % ring) + ring * ring, ring)
+
+    def round_steps(r, chunk):
+        x = partial.at[r]
+        base = r * 2 * ring
+        sib_copies = {}
+        for idx, (s, half) in enumerate((s, half) for s in range(1, ring + 1) for half in (0, 1)):
+            at = need(s, half)
+            sib_copies[(s, half)] = remote(
+                x.at[pl.ds(pl.multiple_of((at * 2 + 1 - c) * m + half * h, 8), h)],
+                sibbuf.at[r, pl.ds(pl.multiple_of(at * m + half * h, 8), h)],
+                sib, sib_sems, base + idx,
+            )
+        yield
+
+        def contribution(s, half):
+            at = need(s, half)
+            sib_copies[(s, half)].wait()
+            own = x[pl.ds(pl.multiple_of((at * 2 + c) * m + half * h, 8), h)]
+            return own + sibbuf[r, pl.ds(pl.multiple_of(at * m + half * h, 8), h)]
+
+        ring_copies = {}
+        for s in range(1, ring):
+            for half in (0, 1):
+                value = contribution(s, half)
+                if s > 1:
+                    ring_copies[(s - 1, half)].wait()
+                    value = value + rbuf[r, half, s - 2]
+                sbuf[r, half, s - 1] = value
+                ring_copies[(s, half)] = remote(
+                    sbuf.at[r, half, s - 1], rbuf.at[r, half, s - 1],
+                    right if half == 0 else left, z_sems, base + half * (ring - 1) + s - 1,
+                )
+            yield
+        for half in (0, 1):
+            value = contribution(ring, half)
+            ring_copies[(ring - 1, half)].wait()
+            out_ref[pl.ds(pl.multiple_of(chunk * m + half * h, 8), h)] = value + rbuf[r, half, ring - 2]
+        yield
+
+    def project(r, src):
+        partial[r] = jnp.dot(src[...], w_ref[...], preferred_element_type=jnp.float32, precision=lax.Precision.HIGH)
+
+    y1r = remote(tok_ref, tg.at[1], y_right, y_sems, 0)
+    y1l = remote(tok_ref, tg.at[2], y_left, y_sems, 1)
+    project(0, tok_ref)
+    rounds = [round_steps(0, y)]
+    next(rounds[0])
+    next(rounds[0])
+    next(rounds[0])
+    y1r.wait()
+    y1l.wait()
+    half_rows = rows // 2
+    y2r = remote(tg.at[1, pl.ds(0, half_rows)], tg.at[3, pl.ds(0, half_rows)], y_right, y_sems, 2)
+    y2l = remote(tg.at[2, pl.ds(half_rows, half_rows)], tg.at[3, pl.ds(half_rows, half_rows)], y_left, y_sems, 3)
+    project(1, tg.at[1])
+    rounds.append(round_steps(1, lax.rem(y + cols - 1, cols)))
+    next(rounds[1])
+    project(2, tg.at[2])
+    rounds.append(round_steps(2, lax.rem(y + 1, cols)))
+    next(rounds[2])
+    for _ in range(2):
+        for g in rounds:
+            next(g, None)
+    y2r.wait()
+    y2l.wait()
+    project(3, tg.at[3])
+    rounds.append(round_steps(3, lax.rem(y + 2, cols)))
+    next(rounds[3])
+    live = list(rounds)
+    while live:
+        live = [g for g in live if next(g, "done") != "done"]
+
+
+def front(tokens, weights, ring, cols, collective_id):
+    rows, width = tokens.shape
+    out_w = weights.shape[1]
+    m = rows // (2 * ring)
+    return pl.pallas_call(
+        functools.partial(front_kernel, ring, cols),
+        out_shape=jax.ShapeDtypeStruct((cols * m, out_w), jnp.float32),
+        in_specs=[pl.BlockSpec(memory_space=pltpu.VMEM), pl.BlockSpec(memory_space=pltpu.VMEM)],
+        out_specs=pl.BlockSpec(memory_space=pltpu.VMEM),
+        scratch_shapes=[
+            pltpu.VMEM((cols, rows, width), jnp.float32),
+            pltpu.VMEM((cols, rows, out_w), jnp.float32),
+            pltpu.VMEM((cols, ring * m, out_w), jnp.float32),
+            pltpu.VMEM((cols, 2, ring - 1, m // 2, out_w), jnp.float32),
+            pltpu.VMEM((cols, 2, ring - 1, m // 2, out_w), jnp.float32),
+            (pltpu.SemaphoreType.DMA((4,)), pltpu.SemaphoreType.DMA((4,))),
+            (pltpu.SemaphoreType.DMA((cols * 2 * ring,)), pltpu.SemaphoreType.DMA((cols * 2 * ring,))),
+            (pltpu.SemaphoreType.DMA((cols * 2 * ring,)), pltpu.SemaphoreType.DMA((cols * 2 * ring,))),
+        ],
+        compiler_params=pltpu.CompilerParams(
+            collective_id=collective_id, has_side_effects=True, vmem_limit_bytes=60 * 1024 * 1024
+        ),
+    )(tokens, weights)
+
+
 def on_device(ring, cols, tokens, w_query, w_key, w_value, w_out):
     highest = lax.Precision.HIGH
-    gathered = ring_gather(tokens, "col", cols, False, 2)
     q_width = w_query.shape[1]
     kv_width = w_key.shape[1]
-
-    def product(weight):
-        return jnp.dot(gathered, weight, preferred_element_type=jnp.float32, precision=highest)
-
-    partial = product(jnp.concatenate([w_query, w_key, w_value], axis=1))
-    joined = ring_scatter(partial, "rz", ring, True, 4, 3)
+    joined = front(tokens, jnp.concatenate([w_query, w_key, w_value], axis=1), ring, cols, 3)
     query_rows = joined[:, :q_width]
     all_kv = ring_gather(joined[:, q_width:], "rz", ring, True, 0)
     state_end = fold_keys(

time: 250 us -> 204 us (0.82)
  Pallas kernels: 221 us -> 183 us
  matrix products: 22.1 us -> 8.82 us
  other arithmetic: 1.37 us -> 4.87 us
    pallas_call x2 -> x1, Pallas kernels: 62.6 us -> 23.4 us  [ring_gather(): pl.pallas_call(functools.partial(gather_kernel, axis, ring, n, with_sib),...]
    pallas_call x1, Pallas kernels: 64.8 us -> 91.8 us  [front(): pl.pallas_call(functools.partial(front_kernel, ring, cols), out_shape=jax...]
    pallas_call x1, Pallas kernels: 93.5 us -> 68.2 us  [gather_mix(): pl.pallas_call(functools.partial(mix_kernel, ring, cols, n), out_shape=ja...]
    dot_general x1 -> x0, matrix products: 13.3 us -> none  [product(): jnp.dot(gathered, weight, preferred_element_type=jnp.float32, precision=h...]
    concatenate x0 -> x1, other arithmetic: none -> 3.5 us  [on_device(): jnp.concatenate([w_query, w_key, w_value], axis=1)]
where the time goes in v6:
time: 204 us; the launch traced here: 202 us
  Pallas kernels  183 us (90%)
  matrix products  8.82 us (4%)
  other arithmetic  4.87 us (2%)
  local copies, waits for them, and re-layouts  4.83 us (2%)
    pallas_call x1, Pallas kernels, front(): pl.pallas_call(functools.partial(front_kernel, ring, cols), out_shape=jax...  91.8 us
    pallas_call x1, Pallas kernels, gather_mix(): pl.pallas_call(functools.partial(mix_kernel, ring, cols, n), out_shape=ja...  68.2 us
    pallas_call x1, Pallas kernels, ring_gather(): pl.pallas_call(functools.partial(gather_kernel, axis, ring, n, with_sib),...  23.4 us
    dot_general x1, matrix products, fold_keys(): jnp.einsum('rkgd,nkd->kgrn', query_head_rows, key_head_rows, precision=hi...  5.37 us

profile of v6, /device:TPU:22, one launch (start us, length us, event | category | flops | bytes accessed | tf_op | source)
XLA Modules:
  0.0 201.9 jit_solution(2044749409906811224)
XLA Ops:
  0.0 3.5 %pad_maximum_fusion.w_ref = f32[512,1280]{1,0:T(8,128)} fusion(f32[512,128]{1,0:T(8,128)} %param.8, f32[512,128]{1,0:T(8,128)} %param.7, f32[512,1024]{1,0:T(8,128)} %param.6), kind=kLoop, calls=%fused_computation.8 | loop fusion | flops 1310720 | bytes 5242880 | tf_op jit(solution)/shard_map/concatenate | solution.py:520
  3.5 91.8 %shard_map.55 = f32[128,1280]{1,0:T(8,128)} custom-call(f32[512,512]{1,0:T(8,128)} %tok_ref.1, f32[512,1280]{1,0:T(8,128)} %pad_maximum_fusion.w_ref), custom_call_target="tpu_custom_call" | custom-call | tf_op jit(solution)/shard_map/pallas_call | solution.py:495
  95.3 1.6 slice.12.x_ref
  96.9 23.4 %shard_map.56 = f32[2048,256]{1,0:T(8,128)} custom-call(f32[128,256]{1,0:T(8,128)} %slice.12.x_ref), custom_call_target="tpu_custom_call" | custom-call | tf_op jit(solution)/shard_map/pallas_call | solution.py:129
  120.3 0.0 copy-start
  120.3 5.4 %bitcast_reduce_fusion = (f32[8,128]{1,0:T(8,128)S(1)}, f32[2048,128,8]{1,0,2:T(8,128)S(1)}) fusion(f32[2048,256]{1,0:T(8,128)} %shard_map.56, f32[128,1280]{1,0:T(8,128)} %shard_map.55), kind=kOutput, calls=%fused_computation.3 | convolution fusion | flops 1614806016 | bytes 9965568 | tf_op jit(solution)/shard_map/rkgd,nkd->kgrn/dot_general | solution.py:40
  125.7 1.4 fusion.3
  127.0 0.0 copy-done
  127.0 3.5 %fusion.12 = f32[8,128,128]{1,2,0:T(8,128)S(1)} fusion(f32[2048,256]{1,0:T(8,128)S(1)} %copy-done, f32[2048,128,8]{1,0,2:T(8,128)S(1)} %get-tuple-element.6, f32[8,128]{1,0:T(8,128)S(1)} %broadcast_maximum_fusion, f32[8,128]{1,0:T(8,128)S(1)} %fusion.3), kind=kOutput, calls=%fused_computation.14 | convolution fusion | flops 1614938112 | bytes 9969664 | tf_op jit(solution)/shard_map/kgrn,nkd->kgrd/dot_general | solution.py:46
  130.5 1.0 copy.13.o_ref
  131.5 68.2 %shard_map.57 = f32[512,512]{1,0:T(8,128)} custom-call(f32[128,1024]{1,0:T(8,128)} %copy.13.o_ref, f32[1024,512]{1,0:T(8,128)} %wo_ref.1), custom_call_target="tpu_custom_call" | custom-call | tf_op jit(solution)/shard_map/pallas_call | solution.py:363
  199.7 2.3 %copy.22 = f32[512,512]{1,0:T(8,128)} copy(f32[512,512]{1,0:T(8,128)} %shard_map.57) | data formatting | bytes 2097152
  (1 shorter events, 0.0 us)
Async XLA Ops:
  120.3 6.8 %copy-start = (f32[2048,256]{1,0:T(8,128)S(1)}, f32[2048,256]{1,0:T(8,128)}, u32[]{:S(2)}) copy-start(f32[2048,256]{1,0:T(8,128)} %shard_map.56) | copy-start | bytes 6291460

commit v7 on v6

--- a/solution.py
+++ b/solution.py
@@ -380,7 +380,10 @@
     )(o, w_out)
 
 
-def front_kernel(ring, cols, tok_ref, w_ref, out_ref, tg, partial, sibbuf, sbuf, rbuf, y_sems, z_sems, sib_sems):
+def front_kernel(
+    ring, cols, tok_ref, wq_ref, wk_ref, wv_ref, out_ref, kv_out, tg, partial, sibbuf, sbuf, rbuf, kvbuf,
+    y_sems, z_sems, sib_sems, kv_sems,
+):
     mesh_id = pl.DeviceIdType.MESH
     names = ("depth", "rz", "rc", "col")
     me = {a: lax.axis_index(a) for a in names}
@@ -451,11 +454,54 @@
         for half in (0, 1):
             value = contribution(ring, half)
             ring_copies[(ring - 1, half)].wait()
-            out_ref[pl.ds(pl.multiple_of(chunk * m + half * h, 8), h)] = value + rbuf[r, half, ring - 2]
+            value = value + rbuf[r, half, ring - 2]
+            out_ref[pl.ds(pl.multiple_of(chunk * m + half * h, 8), h)] = value
+            kvbuf[r, z * 2 + c, pl.ds(half * h, h)] = value[:, qw:]
         yield
 
+        def kv_copy(src, at, lo, size, peer, idx):
+            return remote(src, kvbuf.at[r, at * 2 + c, pl.ds(lo, size)], peer, kv_sems, base + idx)
+
+        kv_sib = [
+            remote(kvbuf.at[r, z * 2 + c], kvbuf.at[r, z * 2 + c], sib, kv_sems, base + ring)
+        ]
+        half_ring = ring // 2
+        for s in range(1, half_ring + 1):
+            origin_r = lax.rem(z - (s - 1) + ring, ring)
+            origin_l = lax.rem(z + (s - 1), ring)
+            src_r = kvbuf.at[r, origin_r * 2 + c]
+            src_l = kvbuf.at[r, origin_l * 2 + c]
+            if s < half_ring:
+                cr = kv_copy(src_r, origin_r, 0, m, right, 2 * (s - 1))
+                cl = kv_copy(src_l, origin_l, 0, m, left, 2 * (s - 1) + 1)
+            else:
+                cr = kv_copy(src_r.at[pl.ds(0, h)], origin_r, 0, h, right, 2 * (s - 1))
+                cl = kv_copy(src_l.at[pl.ds(h, h)], origin_l, h, h, left, 2 * (s - 1) + 1)
+            yield
+            cr.wait()
+            cl.wait()
+            if s < half_ring:
+                got = [(lax.rem(z - s + ring, ring), ring + 2 * s - 1), (lax.rem(z + s, ring), ring + 2 * s)]
+            else:
+                got = [(lax.rem(z + half_ring, ring), ring + 2 * s - 1)]
+            for at, idx in got:
+                kv_sib.append(
+                    remote(kvbuf.at[r, at * 2 + c], kvbuf.at[r, at * 2 + c], sib, kv_sems, base + idx)
+                )
+        yield
+        for cp in kv_sib:
+            cp.wait()
+        yield
+
+    qw = wq_ref.shape[1]
+    kw = wk_ref.shape[1]
+
     def project(r, src):
-        partial[r] = jnp.dot(src[...], w_ref[...], preferred_element_type=jnp.float32, precision=lax.Precision.HIGH)
+        block = src[...]
+        for lo, w_ref in ((0, wq_ref), (qw, wk_ref), (qw + kw, wv_ref)):
+            partial[r, :, pl.ds(lo, w_ref.shape[1])] = jnp.dot(
+                block, w_ref[...], preferred_element_type=jnp.float32, precision=lax.Precision.HIGH
+            )
 
     y1r = remote(tok_ref, tg.at[1], y_right, y_sems, 0)
     y1l = remote(tok_ref, tg.at[2], y_left, y_sems, 1)
@@ -486,40 +532,47 @@
     live = list(rounds)
     while live:
         live = [g for g in live if next(g, "done") != "done"]
-
-
-def front(tokens, weights, ring, cols, collective_id):
+    kv_out[...] = kvbuf[...]
+
+
+def front(tokens, w_query, w_key, w_value, ring, cols, collective_id):
     rows, width = tokens.shape
-    out_w = weights.shape[1]
+    out_w = w_query.shape[1] + w_key.shape[1] + w_value.shape[1]
+    kv_w = w_key.shape[1] + w_value.shape[1]
     m = rows // (2 * ring)
     return pl.pallas_call(
         functools.partial(front_kernel, ring, cols),
-        out_shape=jax.ShapeDtypeStruct((cols * m, out_w), jnp.float32),
-        in_specs=[pl.BlockSpec(memory_space=pltpu.VMEM), pl.BlockSpec(memory_space=pltpu.VMEM)],
-        out_specs=pl.BlockSpec(memory_space=pltpu.VMEM),
+        out_shape=(
+            jax.ShapeDtypeStruct((cols * m, out_w), jnp.float32),
+            jax.ShapeDtypeStruct((cols, 2 * ring, m, kv_w), jnp.float32),
+        ),
+        in_specs=[pl.BlockSpec(memory_space=pltpu.VMEM)] * 4,
+        out_specs=(pl.BlockSpec(memory_space=pltpu.VMEM), pl.BlockSpec(memory_space=pltpu.VMEM)),
         scratch_shapes=[
             pltpu.VMEM((cols, rows, width), jnp.float32),
             pltpu.VMEM((cols, rows, out_w), jnp.float32),
             pltpu.VMEM((cols, ring * m, out_w), jnp.float32),
             pltpu.VMEM((cols, 2, ring - 1, m // 2, out_w), jnp.float32),
             pltpu.VMEM((cols, 2, ring - 1, m // 2, out_w), jnp.float32),
+            pltpu.VMEM((cols, 2 * ring, m, kv_w), jnp.float32),
             (pltpu.SemaphoreType.DMA((4,)), pltpu.SemaphoreType.DMA((4,))),
+            (pltpu.SemaphoreType.DMA((cols * 2 * ring,)), pltpu.SemaphoreType.DMA((cols * 2 * ring,))),
             (pltpu.SemaphoreType.DMA((cols * 2 * ring,)), pltpu.SemaphoreType.DMA((cols * 2 * ring,))),
             (pltpu.SemaphoreType.DMA((cols * 2 * ring,)), pltpu.SemaphoreType.DMA((cols * 2 * ring,))),
         ],
         compiler_params=pltpu.CompilerParams(
             collective_id=collective_id, has_side_effects=True, vmem_limit_bytes=60 * 1024 * 1024
         ),
-    )(tokens, weights)
+    )(tokens, w_query, w_key, w_value)
 
 
 def on_device(ring, cols, tokens, w_query, w_key, w_value, w_out):
     highest = lax.Precision.HIGH
     q_width = w_query.shape[1]
     kv_width = w_key.shape[1]
-    joined = front(tokens, jnp.concatenate([w_query, w_key, w_value], axis=1), ring, cols, 3)
+    joined, kv_sets = front(tokens, w_query, w_key, w_value, ring, cols, 3)
     query_rows = joined[:, :q_width]
-    all_kv = ring_gather(joined[:, q_width:], "rz", ring, True, 0)
+    all_kv = kv_sets.reshape(-1, kv_sets.shape[-1])
     state_end = fold_keys(
         query_rows,
         start_state(query_rows, kv_width),

time: 204 us -> 197 us (0.966)
  other arithmetic: 4.87 us -> 1.37 us
    concatenate x1 -> x0, other arithmetic: 3.5 us -> none  [on_device(): jnp.concatenate([w_query, w_key, w_value], axis=1)]
    pallas_call x2 -> x1, Pallas kernels: 115 us -> 113 us  [front(): pl.pallas_call(functools.partial(front_kernel, ring, cols), out_shape=(ja...]
where the time goes in v7:
time: 197 us; the launch traced here: 195 us
  Pallas kernels  181 us (92%)
  matrix products  8.83 us (4%)
  local copies, waits for them, and re-layouts  3.26 us (2%)
    pallas_call x1, Pallas kernels, front(): pl.pallas_call(functools.partial(front_kernel, ring, cols), out_shape=(ja...  113 us
    pallas_call x1, Pallas kernels, gather_mix(): pl.pallas_call(functools.partial(mix_kernel, ring, cols, n), out_shape=ja...  68.6 us
    dot_general x1, matrix products, fold_keys(): jnp.einsum('rkgd,nkd->kgrn', query_head_rows, key_head_rows, precision=hi...  5.37 us

profile of v7, /device:TPU:22, one launch (start us, length us, event | category | flops | bytes accessed | tf_op | source)
XLA Modules:
  0.0 194.8 jit_solution(12586637180991551098)
XLA Ops:
  0.0 112.7 %shard_map.55 = (f32[128,1280]{1,0:T(8,128)}, f32[4,16,32,256]{3,2,1,0:T(8,128)}) custom-call(f32[512,512]{1,0:T(8,128)} %tok_ref.1, f32[512,1024]{1,0:T(8,128)} %wq_ref.1, f32[512,128]{1,0:T(8,128)} %wk_ref.1, f32[512,128]{1,0:T(8,128)} %wv_ref.1), custom_call_target="tpu_custom_call" | custom-call | tf_op jit(solution)/shard_map/pallas_call | solution.py:543
  112.7 0.0 copy-start
  112.7 5.4 %bitcast_reduce_fusion = (f32[8,128]{1,0:T(8,128)S(1)}, f32[2048,128,8]{1,0,2:T(8,128)S(1)}) fusion(f32[2048,256]{1,0:T(8,128)} %bitcast.45, f32[128,1280]{1,0:T(8,128)} %get-tuple-element.8), kind=kOutput, calls=%fused_computation.3 | convolution fusion | flops 1614806016 | bytes 9965568 | tf_op jit(solution)/shard_map/rkgd,nkd->kgrn/dot_general | solution.py:40
  118.1 1.4 fusion.3
  119.4 0.0 copy-done
  119.5 3.5 %fusion.8 = f32[8,128,128]{1,2,0:T(8,128)S(1)} fusion(f32[2048,256]{1,0:T(8,128)S(1)} %bitcast.46, f32[2048,128,8]{1,0,2:T(8,128)S(1)} %get-tuple-element.10, f32[8,128]{1,0:T(8,128)S(1)} %broadcast_maximum_fusion, f32[8,128]{1,0:T(8,128)S(1)} %fusion.3), kind=kOutput, calls=%fused_computation.11 | convolution fusion | flops 1614938112 | bytes 9969664 | tf_op jit(solution)/shard_map/kgrn,nkd->kgrd/dot_general | solution.py:46
  122.9 1.0 copy.13.o_ref
  123.9 68.6 %shard_map.56 = f32[512,512]{1,0:T(8,128)} custom-call(f32[128,1024]{1,0:T(8,128)} %copy.13.o_ref, f32[1024,512]{1,0:T(8,128)} %wo_ref.1), custom_call_target="tpu_custom_call" | custom-call | tf_op jit(solution)/shard_map/pallas_call | solution.py:363
  192.6 2.3 %copy.22 = f32[512,512]{1,0:T(8,128)} copy(f32[512,512]{1,0:T(8,128)} %shard_map.56) | data formatting | bytes 2097152
  (1 shorter events, 0.0 us)
Async XLA Ops:
  112.7 6.8 %copy-start = (f32[4,16,32,256]{3,2,1,0:T(8,128)S(1)}, f32[4,16,32,256]{3,2,1,0:T(8,128)}, u32[]{:S(2)}) copy-start(f32[4,16,32,256]{3,2,1,0:T(8,128)} %get-tuple-element.7) | copy-start | bytes 6291460

commit v8 on v7

--- a/solution.py
+++ b/solution.py
@@ -507,9 +507,8 @@
     y1l = remote(tok_ref, tg.at[2], y_left, y_sems, 1)
     project(0, tok_ref)
     rounds = [round_steps(0, y)]
-    next(rounds[0])
-    next(rounds[0])
-    next(rounds[0])
+    for _ in range(ring):
+        next(rounds[0])
     y1r.wait()
     y1l.wait()
     half_rows = rows // 2

time: 197 us -> 194 us (0.985)
  Pallas kernels: 181 us -> 179 us
where the time goes in v8:
time: 194 us; the launch traced here: 193 us
  Pallas kernels  179 us (92%)
  matrix products  8.83 us (5%)
  local copies, waits for them, and re-layouts  3.26 us (2%)
    pallas_call x1, Pallas kernels, front(): pl.pallas_call(functools.partial(front_kernel, ring, cols), out_shape=(ja...  111 us
    pallas_call x1, Pallas kernels, gather_mix(): pl.pallas_call(functools.partial(mix_kernel, ring, cols, n), out_shape=ja...  68.3 us
    dot_general x1, matrix products, fold_keys(): jnp.einsum('rkgd,nkd->kgrn', query_head_rows, key_head_rows, precision=hi...  5.37 us

profile of v8, /device:TPU:22, one launch (start us, length us, event | category | flops | bytes accessed | tf_op | source)
XLA Modules:
  0.0 192.6 jit_solution(4295976486260833546)
XLA Ops:
  0.0 110.8 %shard_map.55 = (f32[128,1280]{1,0:T(8,128)}, f32[4,16,32,256]{3,2,1,0:T(8,128)}) custom-call(f32[512,512]{1,0:T(8,128)} %tok_ref.1, f32[512,1024]{1,0:T(8,128)} %wq_ref.1, f32[512,128]{1,0:T(8,128)} %wk_ref.1, f32[512,128]{1,0:T(8,128)} %wv_ref.1), custom_call_target="tpu_custom_call" | custom-call | tf_op jit(solution)/shard_map/pallas_call | solution.py:542
  110.8 0.0 copy-start
  110.8 5.4 %bitcast_reduce_fusion = (f32[8,128]{1,0:T(8,128)S(1)}, f32[2048,128,8]{1,0,2:T(8,128)S(1)}) fusion(f32[2048,256]{1,0:T(8,128)} %bitcast.45, f32[128,1280]{1,0:T(8,128)} %get-tuple-element.8), kind=kOutput, calls=%fused_computation.3 | convolution fusion | flops 1614806016 | bytes 9965568 | tf_op jit(solution)/shard_map/rkgd,nkd->kgrn/dot_general | solution.py:40
  116.2 1.4 fusion.3
  117.6 0.0 copy-done
  117.6 3.5 %fusion.8 = f32[8,128,128]{1,2,0:T(8,128)S(1)} fusion(f32[2048,256]{1,0:T(8,128)S(1)} %bitcast.46, f32[2048,128,8]{1,0,2:T(8,128)S(1)} %get-tuple-element.10, f32[8,128]{1,0:T(8,128)S(1)} %broadcast_maximum_fusion, f32[8,128]{1,0:T(8,128)S(1)} %fusion.3), kind=kOutput, calls=%fused_computation.11 | convolution fusion | flops 1614938112 | bytes 9969664 | tf_op jit(solution)/shard_map/kgrn,nkd->kgrd/dot_general | solution.py:46
  121.0 1.0 copy.13.o_ref
  122.0 68.3 %shard_map.56 = f32[512,512]{1,0:T(8,128)} custom-call(f32[128,1024]{1,0:T(8,128)} %copy.13.o_ref, f32[1024,512]{1,0:T(8,128)} %wo_ref.1), custom_call_target="tpu_custom_call" | custom-call | tf_op jit(solution)/shard_map/pallas_call | solution.py:363
  190.3 2.3 %copy.22 = f32[512,512]{1,0:T(8,128)} copy(f32[512,512]{1,0:T(8,128)} %shard_map.56) | data formatting | bytes 2097152
  (1 shorter events, 0.0 us)
Async XLA Ops:
  110.8 6.8 %copy-start = (f32[4,16,32,256]{3,2,1,0:T(8,128)S(1)}, f32[4,16,32,256]{3,2,1,0:T(8,128)}, u32[]{:S(2)}) copy-start(f32[4,16,32,256]{3,2,1,0:T(8,128)} %get-tuple-element.7) | copy-start | bytes 6291460

commit v9 on v8

--- a/solution.py
+++ b/solution.py
@@ -253,12 +253,16 @@
     )(x)
 
 
-def mix_kernel(ring, cols, n, o_ref, wo_ref, out_ref, ogath, part, recv, send_sems, recv_sems, y_send, y_recv):
+def mix_kernel(
+    ring, cols, n, o_ref, wo_ref, out_ref, ogath, part, fwd_a, fwd_b, comb_l, comb_r, recv_l, recv_r,
+    send_sems, recv_sems, fa_sems, fb_sems, cl_sems, cr_sems,
+):
     mesh_id = pl.DeviceIdType.MESH
     names = ("depth", "rz", "rc", "col")
     me = {a: lax.axis_index(a) for a in names}
     z, c, y = me["rz"], me["rc"], me["col"]
-    per_col = 2 * ring // cols
+    piece = n // cols
+    hp = piece // 2
 
     def device(**moved):
         return tuple(moved.get(a, me[a]) for a in names)
@@ -266,39 +270,54 @@
     right = device(rz=lax.rem(z + 1, ring))
     left = device(rz=lax.rem(z + ring - 1, ring))
     sib = device(rc=1 - c)
-    peers = [left, right, sib] + [device(col=lax.rem(y + d, cols)) for d in range(1, cols)]
+    y_l = lax.rem(y + cols - 1, cols)
+    y_r = lax.rem(y + 1, cols)
+    y_o = lax.rem(y + 2, cols)
+    peers = [left, right, sib, device(col=y_l), device(col=y_r)]
 
     barrier = pltpu.get_barrier_semaphore()
     for peer in peers:
         pl.semaphore_signal(barrier, inc=1, device_id=peer, device_id_type=mesh_id)
     pl.semaphore_wait(barrier, len(peers))
 
-    def remote(src, dst, peer, send, recv_sem):
+    def remote(src, dst, peer, sems, idx):
         cp = pltpu.make_async_remote_copy(
-            src_ref=src, dst_ref=dst, send_sem=send, recv_sem=recv_sem, device_id=peer, device_id_type=mesh_id
+            src_ref=src, dst_ref=dst, send_sem=sems[0].at[idx], recv_sem=sems[1].at[idx],
+            device_id=peer, device_id_type=mesh_id,
         )
         cp.start()
         return cp
 
-    piece = n // cols
+    def rows_at(p, lo, size):
+        return pl.ds(pl.multiple_of(p * piece + lo, 8), size)
+
+    y_copies = []
+    pending = []
+
+    def combine(k, fa, fb):
+        fa.wait_recv()
+        comb_l[k, pl.ds(0, hp)] = part[k, rows_at(y_l, 0, hp)] + fwd_a[k]
+        comb_l[k, pl.ds(hp, hp)] = part[k, rows_at(y_l, hp, hp)]
+        y_copies.append(remote(comb_l.at[k], recv_r.at[k], device(col=y_l), cl_sems, k))
+        fb.wait_recv()
+        comb_r[k, pl.ds(0, hp)] = part[k, rows_at(y_r, 0, hp)]
+        comb_r[k, pl.ds(hp, hp)] = part[k, rows_at(y_r, hp, hp)] + fwd_b[k]
+        y_copies.append(remote(comb_r.at[k], recv_l.at[k], device(col=y_r), cr_sems, k))
 
     def project(block, k):
         part[k] = jnp.dot(block, wo_ref[...], preferred_element_type=jnp.float32, precision=lax.Precision.HIGH)
-        for d in range(1, cols):
-            dest = lax.rem(y + d, cols)
-            remote(
-                part.at[k, pl.ds(pl.multiple_of(dest * piece, 8), piece)],
-                recv.at[cols - d, k],
-                device(col=dest),
-                y_send.at[k * cols + d],
-                y_recv.at[(cols - d) * 2 * ring + k],
-            )
+        fa = remote(part.at[k, rows_at(y_o, 0, hp)], fwd_a.at[k], device(col=y_l), fa_sems, k)
+        fb = remote(part.at[k, rows_at(y_o, hp, hp)], fwd_b.at[k], device(col=y_r), fb_sems, k)
+        y_copies.extend([fa, fb])
+        while pending:
+            combine(*pending.pop(0))
+        pending.append((k, fa, fb))
 
     def slot(zz, cc):
         return zz * 2 + cc
 
     def z_copy(src, dst_slot, lo, size, peer, idx):
-        return remote(src, ogath.at[dst_slot, pl.ds(lo, size)], peer, send_sems.at[idx], recv_sems.at[idx])
+        return remote(src, ogath.at[dst_slot, pl.ds(lo, size)], peer, (send_sems, recv_sems), idx)
 
     project(o_ref[...], slot(z, c))
     pending_sib = [(z_copy(o_ref, slot(z, c), 0, n, sib, ring), z)]
@@ -331,48 +350,45 @@
     for cp, at in pending_sib:
         cp.wait()
         project(ogath[slot(at, 1 - c)], slot(at, 1 - c))
+    while pending:
+        combine(*pending.pop(0))
     for k in range(2 * ring):
-        total = part[k, pl.ds(pl.multiple_of(y * piece, 8), piece)]
-        for d in range(1, cols):
+        for buf, sems, peer in ((recv_l, cr_sems, device(col=y_l)), (recv_r, cl_sems, device(col=y_r))):
             pltpu.make_async_remote_copy(
-                src_ref=part.at[k, pl.ds(0, piece)],
-                dst_ref=recv.at[d, k],
-                send_sem=y_send.at[0],
-                recv_sem=y_recv.at[d * 2 * ring + k],
-                device_id=device(col=lax.rem(y + d, cols)),
-                device_id_type=mesh_id,
+                src_ref=comb_l.at[k], dst_ref=buf.at[k], send_sem=sems[0].at[k], recv_sem=sems[1].at[k],
+                device_id=peer, device_id_type=mesh_id,
             ).wait_recv()
-            total = total + recv[d, k]
-        out_ref[pl.ds(k * piece, piece)] = total
-    for k in range(2 * ring):
-        for d in range(1, cols):
-            pltpu.make_async_remote_copy(
-                src_ref=part.at[k, pl.ds(0, piece)],
-                dst_ref=recv.at[0, 0],
-                send_sem=y_send.at[k * cols + d],
-                recv_sem=y_recv.at[0],
-                device_id=device(col=lax.rem(y + d, cols)),
-                device_id_type=mesh_id,
-            ).wait_send()
+        out_ref[pl.ds(k * piece, piece)] = part[k, rows_at(y, 0, piece)] + recv_l[k] + recv_r[k]
+    for cp in y_copies:
+        cp.wait_send()
 
 
 def gather_mix(o, w_out, ring, cols, collective_id):
     n, width = o.shape
     out_w = w_out.shape[1]
-    per_col = 2 * ring // cols
+    piece = n // cols
+    slots = 2 * ring
+
+    def sems():
+        return (pltpu.SemaphoreType.DMA((slots,)), pltpu.SemaphoreType.DMA((slots,)))
+
     return pl.pallas_call(
         functools.partial(mix_kernel, ring, cols, n),
-        out_shape=jax.ShapeDtypeStruct((per_col * n, out_w), jnp.float32),
+        out_shape=jax.ShapeDtypeStruct((slots * piece, out_w), jnp.float32),
         in_specs=[pl.BlockSpec(memory_space=pltpu.VMEM), pl.BlockSpec(memory_space=pltpu.VMEM)],
         out_specs=pl.BlockSpec(memory_space=pltpu.VMEM),
         scratch_shapes=[
-            pltpu.VMEM((2 * ring, n, width), jnp.float32),
-            pltpu.VMEM((2 * ring, n, out_w), jnp.float32),
-            pltpu.VMEM((cols, 2 * ring, n // cols, out_w), jnp.float32),
-            pltpu.SemaphoreType.DMA((2 * ring,)),
-            pltpu.SemaphoreType.DMA((2 * ring,)),
-            pltpu.SemaphoreType.DMA((2 * ring * cols,)),
-            pltpu.SemaphoreType.DMA((2 * ring * cols,)),
+            pltpu.VMEM((slots, n, width), jnp.float32),
+            pltpu.VMEM((slots, n, out_w), jnp.float32),
+            pltpu.VMEM((slots, piece // 2, out_w), jnp.float32),
+            pltpu.VMEM((slots, piece // 2, out_w), jnp.float32),
+            pltpu.VMEM((slots, piece, out_w), jnp.float32),
+            pltpu.VMEM((slots, piece, out_w), jnp.float32),
+            pltpu.VMEM((slots, piece, out_w), jnp.float32),
+            pltpu.VMEM((slots, piece, out_w), jnp.float32),
+            pltpu.SemaphoreType.DMA((slots,)),
+            pltpu.SemaphoreType.DMA((slots,)),
+            sems(), sems(), sems(), sems(),
         ],
         compiler_params=pltpu.CompilerParams(
             collective_id=collective_id, has_side_effects=True, vmem_limit_bytes=60 * 1024 * 1024

time: 194 us -> 198 us (1.021)
  Pallas kernels: 179 us -> 183 us
    pallas_call x1, Pallas kernels: 68.3 us -> 71.9 us  [gather_mix(): pl.pallas_call(functools.partial(mix_kernel, ring, cols, n), out_shape=ja...]
where the time goes in v9:
time: 198 us; the launch traced here: 196 us
  Pallas kernels  183 us (92%)
  matrix products  8.83 us (4%)
  local copies, waits for them, and re-layouts  3.26 us (2%)
    pallas_call x1, Pallas kernels, front(): pl.pallas_call(functools.partial(front_kernel, ring, cols), out_shape=(ja...  111 us
    pallas_call x1, Pallas kernels, gather_mix(): pl.pallas_call(functools.partial(mix_kernel, ring, cols, n), out_shape=ja...  71.9 us
    dot_general x1, matrix products, fold_keys(): jnp.einsum('rkgd,nkd->kgrn', query_head_rows, key_head_rows, precision=hi...  5.37 us

profile of v9, /device:TPU:22, one launch (start us, length us, event | category | flops | bytes accessed | tf_op | source)
XLA Modules:
  0.0 196.2 jit_solution(8742450643751593144)
XLA Ops:
  0.0 110.8 %shard_map.55 = (f32[128,1280]{1,0:T(8,128)}, f32[4,16,32,256]{3,2,1,0:T(8,128)}) custom-call(f32[512,512]{1,0:T(8,128)} %tok_ref.1, f32[512,1024]{1,0:T(8,128)} %wq_ref.1, f32[512,128]{1,0:T(8,128)} %wk_ref.1, f32[512,128]{1,0:T(8,128)} %wv_ref.1), custom_call_target="tpu_custom_call" | custom-call | tf_op jit(solution)/shard_map/pallas_call | solution.py:558
  110.8 0.0 copy-start
  110.8 5.4 %bitcast_reduce_fusion = (f32[8,128]{1,0:T(8,128)S(1)}, f32[2048,128,8]{1,0,2:T(8,128)S(1)}) fusion(f32[2048,256]{1,0:T(8,128)} %bitcast.45, f32[128,1280]{1,0:T(8,128)} %get-tuple-element.8), kind=kOutput, calls=%fused_computation.3 | convolution fusion | flops 1614806016 | bytes 9965568 | tf_op jit(solution)/shard_map/rkgd,nkd->kgrn/dot_general | solution.py:40
  116.2 1.4 fusion.3
  117.6 0.0 copy-done
  117.6 3.5 %fusion.8 = f32[8,128,128]{1,2,0:T(8,128)S(1)} fusion(f32[2048,256]{1,0:T(8,128)S(1)} %bitcast.46, f32[2048,128,8]{1,0,2:T(8,128)S(1)} %get-tuple-element.10, f32[8,128]{1,0:T(8,128)S(1)} %broadcast_maximum_fusion, f32[8,128]{1,0:T(8,128)S(1)} %fusion.3), kind=kOutput, calls=%fused_computation.11 | convolution fusion | flops 1614938112 | bytes 9969664 | tf_op jit(solution)/shard_map/kgrn,nkd->kgrd/dot_general | solution.py:46
  121.0 1.0 copy.13.o_ref
  122.0 71.9 %shard_map.56 = f32[512,512]{1,0:T(8,128)} custom-call(f32[128,1024]{1,0:T(8,128)} %copy.13.o_ref, f32[1024,512]{1,0:T(8,128)} %wo_ref.1), custom_call_target="tpu_custom_call" | custom-call | tf_op jit(solution)/shard_map/pallas_call | solution.py:375
  194.0 2.3 %copy.22 = f32[512,512]{1,0:T(8,128)} copy(f32[512,512]{1,0:T(8,128)} %shard_map.56) | data formatting | bytes 2097152
  (1 shorter events, 0.0 us)
Async XLA Ops:
  110.8 6.8 %copy-start = (f32[4,16,32,256]{3,2,1,0:T(8,128)S(1)}, f32[4,16,32,256]{3,2,1,0:T(8,128)}, u32[]{:S(2)}) copy-start(f32[4,16,32,256]{3,2,1,0:T(8,128)} %get-tuple-element.7) | copy-start | bytes 6291460

commit v10 on v8

--- a/solution.py
+++ b/solution.py
@@ -300,8 +300,8 @@
     def z_copy(src, dst_slot, lo, size, peer, idx):
         return remote(src, ogath.at[dst_slot, pl.ds(lo, size)], peer, send_sems.at[idx], recv_sems.at[idx])
 
-    project(o_ref[...], slot(z, c))
     pending_sib = [(z_copy(o_ref, slot(z, c), 0, n, sib, ring), z)]
+    to_project = [slot(z, c)]
     half = ring // 2
     for s in range(1, half + 1):
         origin_r = lax.rem(z - (s - 1) + ring, ring)
@@ -315,6 +315,9 @@
             h = n // 2
             cr = z_copy(src_r.at[pl.ds(0, h)], slot(origin_r, c), 0, h, right, 2 * (s - 1))
             cl = z_copy(src_l.at[pl.ds(h, h)], slot(origin_l, c), h, h, left, 2 * (s - 1) + 1)
+        for k in to_project:
+            project(o_ref[...] if s == 1 else ogath[k], k)
+        to_project = []
         for cp, at in pending_sib:
             cp.wait()
             project(ogath[slot(at, 1 - c)], slot(at, 1 - c))
@@ -327,7 +330,9 @@
             arrived = [(lax.rem(z + half, ring), ring + 2 * s - 1)]
         for at, idx in arrived:
             pending_sib.append((z_copy(ogath.at[slot(at, c)], slot(at, c), 0, n, sib, idx), at))
-            project(ogath[slot(at, c)], slot(at, c))
+            to_project.append(slot(at, c))
+    for k in to_project:
+        project(ogath[k], k)
     for cp, at in pending_sib:
         cp.wait()
         project(ogath[slot(at, 1 - c)], slot(at, 1 - c))

time: 194 us -> 190 us (0.979)
  Pallas kernels: 179 us -> 175 us
    pallas_call x1, Pallas kernels: 68.3 us -> 64.6 us  [gather_mix(): pl.pallas_call(functools.partial(mix_kernel, ring, cols, n), out_shape=ja...]
where the time goes in v10:
time: 190 us; the launch traced here: 189 us
  Pallas kernels  175 us (92%)
  matrix products  8.83 us (5%)
  local copies, waits for them, and re-layouts  3.26 us (2%)
    pallas_call x1, Pallas kernels, front(): pl.pallas_call(functools.partial(front_kernel, ring, cols), out_shape=(ja...  111 us
    pallas_call x1, Pallas kernels, gather_mix(): pl.pallas_call(functools.partial(mix_kernel, ring, cols, n), out_shape=ja...  64.6 us
    dot_general x1, matrix products, fold_keys(): jnp.einsum('rkgd,nkd->kgrn', query_head_rows, key_head_rows, precision=hi...  5.37 us

profile of v10, /device:TPU:22, one launch (start us, length us, event | category | flops | bytes accessed | tf_op | source)
XLA Modules:
  0.0 188.9 jit_solution(10484628090807839096)
XLA Ops:
  0.0 110.8 %shard_map.55 = (f32[128,1280]{1,0:T(8,128)}, f32[4,16,32,256]{3,2,1,0:T(8,128)}) custom-call(f32[512,512]{1,0:T(8,128)} %tok_ref.1, f32[512,1024]{1,0:T(8,128)} %wq_ref.1, f32[512,128]{1,0:T(8,128)} %wk_ref.1, f32[512,128]{1,0:T(8,128)} %wv_ref.1), custom_call_target="tpu_custom_call" | custom-call | tf_op jit(solution)/shard_map/pallas_call | solution.py:547
  110.8 0.0 copy-start
  110.8 5.4 %bitcast_reduce_fusion = (f32[8,128]{1,0:T(8,128)S(1)}, f32[2048,128,8]{1,0,2:T(8,128)S(1)}) fusion(f32[2048,256]{1,0:T(8,128)} %bitcast.45, f32[128,1280]{1,0:T(8,128)} %get-tuple-element.8), kind=kOutput, calls=%fused_computation.3 | convolution fusion | flops 1614806016 | bytes 9965568 | tf_op jit(solution)/shard_map/rkgd,nkd->kgrn/dot_general | solution.py:40
  116.2 1.4 fusion.3
  117.6 0.0 copy-done
  117.6 3.5 %fusion.8 = f32[8,128,128]{1,2,0:T(8,128)S(1)} fusion(f32[2048,256]{1,0:T(8,128)S(1)} %bitcast.46, f32[2048,128,8]{1,0,2:T(8,128)S(1)} %get-tuple-element.10, f32[8,128]{1,0:T(8,128)S(1)} %broadcast_maximum_fusion, f32[8,128]{1,0:T(8,128)S(1)} %fusion.3), kind=kOutput, calls=%fused_computation.11 | convolution fusion | flops 1614938112 | bytes 9969664 | tf_op jit(solution)/shard_map/kgrn,nkd->kgrd/dot_general | solution.py:46
  121.0 1.0 copy.13.o_ref
  122.0 64.6 %shard_map.56 = f32[512,512]{1,0:T(8,128)} custom-call(f32[128,1024]{1,0:T(8,128)} %copy.13.o_ref, f32[1024,512]{1,0:T(8,128)} %wo_ref.1), custom_call_target="tpu_custom_call" | custom-call | tf_op jit(solution)/shard_map/pallas_call | solution.py:368
  186.6 2.3 %copy.22 = f32[512,512]{1,0:T(8,128)} copy(f32[512,512]{1,0:T(8,128)} %shard_map.56) | data formatting | bytes 2097152
  (1 shorter events, 0.0 us)
Async XLA Ops:
  110.8 6.8 %copy-start = (f32[4,16,32,256]{3,2,1,0:T(8,128)S(1)}, f32[4,16,32,256]{3,2,1,0:T(8,128)}, u32[]{:S(2)}) copy-start(f32[4,16,32,256]{3,2,1,0:T(8,128)} %get-tuple-element.7) | copy-start | bytes 6291460

commit v11 on v10

--- a/solution.py
+++ b/solution.py
@@ -348,7 +348,9 @@
                 device_id_type=mesh_id,
             ).wait_recv()
             total = total + recv[d, k]
-        out_ref[pl.ds(k * piece, piece)] = total
+        m = piece // 2
+        for e in (0, 1):
+            out_ref[pl.ds(e * 2 * ring * m + k * m, m)] = total[e * m : (e + 1) * m]
     for k in range(2 * ring):
         for d in range(1, cols):
             pltpu.make_async_remote_copy(
@@ -394,7 +396,7 @@
     me = {a: lax.axis_index(a) for a in names}
     z, c, y = me["rz"], me["rc"], me["col"]
     rows = tok_ref.shape[0]
-    m = rows // (2 * ring)
+    m = rows // 2 // (2 * ring)
     h = m // 2
 
     def device(**moved):
@@ -508,31 +510,49 @@
                 block, w_ref[...], preferred_element_type=jnp.float32, precision=lax.Precision.HIGH
             )
 
-    y1r = remote(tok_ref, tg.at[1], y_right, y_sems, 0)
-    y1l = remote(tok_ref, tg.at[2], y_left, y_sems, 1)
-    project(0, tok_ref)
-    rounds = [round_steps(0, y)]
-    for _ in range(ring):
-        next(rounds[0])
-    y1r.wait()
-    y1l.wait()
-    half_rows = rows // 2
-    y2r = remote(tg.at[1, pl.ds(0, half_rows)], tg.at[3, pl.ds(0, half_rows)], y_right, y_sems, 2)
-    y2l = remote(tg.at[2, pl.ds(half_rows, half_rows)], tg.at[3, pl.ds(half_rows, half_rows)], y_left, y_sems, 3)
-    project(1, tg.at[1])
-    rounds.append(round_steps(1, lax.rem(y + cols - 1, cols)))
-    next(rounds[1])
-    project(2, tg.at[2])
-    rounds.append(round_steps(2, lax.rem(y + 1, cols)))
-    next(rounds[2])
-    for _ in range(2):
-        for g in rounds:
-            next(g, None)
+    hr = rows // 2
+    chunks = (y, lax.rem(y + cols - 1, cols), lax.rem(y + 1, cols), lax.rem(y + 2, cols))
+
+    def sub(ref, e):
+        return ref.at[pl.ds(e * hr, hr)]
+
+    y1 = {}
+    for e in (0, 1):
+        y1[("r", e)] = remote(sub(tok_ref, e), sub(tg.at[1], e), y_right, y_sems, 2 * e)
+        y1[("l", e)] = remote(sub(tok_ref, e), sub(tg.at[2], e), y_left, y_sems, 2 * e + 1)
+    rounds = []
+
+    def begin(slot_id, e, src):
+        r = 2 * slot_id + e
+        project(r, src)
+        g = round_steps(r, 2 * chunks[slot_id] + e)
+        next(g)
+        rounds.append(g)
+
+    def advance(times):
+        for _ in range(times):
+            for g in list(rounds):
+                next(g, None)
+
+    begin(0, 0, sub(tok_ref, 0))
+    begin(0, 1, sub(tok_ref, 1))
+    advance(ring // 2)
+    y1[("r", 0)].wait()
+    y2r = remote(sub(tg.at[1], 0), sub(tg.at[3], 0), y_right, y_sems, 4)
+    y1[("l", 0)].wait()
+    begin(1, 0, sub(tg.at[1], 0))
+    begin(2, 0, sub(tg.at[2], 0))
+    advance(2)
+    y1[("r", 1)].wait()
+    y1[("l", 1)].wait()
+    y2l = remote(sub(tg.at[2], 1), sub(tg.at[3], 1), y_left, y_sems, 5)
+    begin(1, 1, sub(tg.at[1], 1))
+    begin(2, 1, sub(tg.at[2], 1))
+    advance(2)
     y2r.wait()
+    begin(3, 0, sub(tg.at[3], 0))
     y2l.wait()
-    project(3, tg.at[3])
-    rounds.append(round_steps(3, lax.rem(y + 2, cols)))
-    next(rounds[3])
+    begin(3, 1, sub(tg.at[3], 1))
     live = list(rounds)
     while live:
         live = [g for g in live if next(g, "done") != "done"]
@@ -543,26 +563,28 @@
     rows, width = tokens.shape
     out_w = w_query.shape[1] + w_key.shape[1] + w_value.shape[1]
     kv_w = w_key.shape[1] + w_value.shape[1]
-    m = rows // (2 * ring)
+    n_rounds = 2 * cols
+    hr = rows // 2
+    m = hr // (2 * ring)
     return pl.pallas_call(
         functools.partial(front_kernel, ring, cols),
         out_shape=(
-            jax.ShapeDtypeStruct((cols * m, out_w), jnp.float32),
-            jax.ShapeDtypeStruct((cols, 2 * ring, m, kv_w), jnp.float32),
+            jax.ShapeDtypeStruct((n_rounds * m, out_w), jnp.float32),
+            jax.ShapeDtypeStruct((n_rounds, 2 * ring, m, kv_w), jnp.float32),
         ),
         in_specs=[pl.BlockSpec(memory_space=pltpu.VMEM)] * 4,
         out_specs=(pl.BlockSpec(memory_space=pltpu.VMEM), pl.BlockSpec(memory_space=pltpu.VMEM)),
         scratch_shapes=[
             pltpu.VMEM((cols, rows, width), jnp.float32),
-            pltpu.VMEM((cols, rows, out_w), jnp.float32),
-            pltpu.VMEM((cols, ring * m, out_w), jnp.float32),
-            pltpu.VMEM((cols, 2, ring - 1, m // 2, out_w), jnp.float32),
-            pltpu.VMEM((cols, 2, ring - 1, m // 2, out_w), jnp.float32),
-            pltpu.VMEM((cols, 2 * ring, m, kv_w), jnp.float32),
-            (pltpu.SemaphoreType.DMA((4,)), pltpu.SemaphoreType.DMA((4,))),
-            (pltpu.SemaphoreType.DMA((cols * 2 * ring,)), pltpu.SemaphoreType.DMA((cols * 2 * ring,))),
-            (pltpu.SemaphoreType.DMA((cols * 2 * ring,)), pltpu.SemaphoreType.DMA((cols * 2 * ring,))),
-            (pltpu.SemaphoreType.DMA((cols * 2 * ring,)), pltpu.SemaphoreType.DMA((cols * 2 * ring,))),
+            pltpu.VMEM((n_rounds, hr, out_w), jnp.float32),
+            pltpu.VMEM((n_rounds, ring * m, out_w), jnp.float32),
+            pltpu.VMEM((n_rounds, 2, ring - 1, m // 2, out_w), jnp.float32),
+            pltpu.VMEM((n_rounds, 2, ring - 1, m // 2, out_w), jnp.float32),
+            pltpu.VMEM((n_rounds, 2 * ring, m, kv_w), jnp.float32),
+            (pltpu.SemaphoreType.DMA((6,)), pltpu.SemaphoreType.DMA((6,))),
+            (pltpu.SemaphoreType.DMA((n_rounds * 2 * ring,)), pltpu.SemaphoreType.DMA((n_rounds * 2 * ring,))),
+            (pltpu.SemaphoreType.DMA((n_rounds * 2 * ring,)), pltpu.SemaphoreType.DMA((n_rounds * 2 * ring,))),
+            (pltpu.SemaphoreType.DMA((n_rounds * 2 * ring,)), pltpu.SemaphoreType.DMA((n_rounds * 2 * ring,))),
         ],
         compiler_params=pltpu.CompilerParams(
             collective_id=collective_id, has_side_effects=True, vmem_limit_bytes=60 * 1024 * 1024

time: 190 us -> 187 us (0.984)
  Pallas kernels: 175 us -> 171 us
    pallas_call x1, Pallas kernels: 111 us -> 106 us  [front(): pl.pallas_call(functools.partial(front_kernel, ring, cols), out_shape=(ja...]
where the time goes in v11:
time: 187 us; the launch traced here: 185 us
  Pallas kernels  171 us (91%)
  matrix products  9.05 us (5%)
  local copies, waits for them, and re-layouts  3.26 us (2%)
    pallas_call x1, Pallas kernels, front(): pl.pallas_call(functools.partial(front_kernel, ring, cols), out_shape=(ja...  106 us
    pallas_call x1, Pallas kernels, gather_mix(): pl.pallas_call(functools.partial(mix_kernel, ring, cols, n), out_shape=ja...  65.1 us
    dot_general x1, matrix products, fold_keys(): jnp.einsum('rkgd,nkd->kgrn', query_head_rows, key_head_rows, precision=hi...  5.37 us

profile of v11, /device:TPU:22, one launch (start us, length us, event | category | flops | bytes accessed | tf_op | source)
XLA Modules:
  0.0 185.2 jit_solution(7052159185918769170)
XLA Ops:
  0.0 106.3 %shard_map.55 = (f32[128,1280]{1,0:T(8,128)}, f32[8,16,16,256]{3,2,1,0:T(8,128)}) custom-call(f32[512,512]{1,0:T(8,128)} %tok_ref.1, f32[512,1024]{1,0:T(8,128)} %wq_ref.1, f32[512,128]{1,0:T(8,128)} %wk_ref.1, f32[512,128]{1,0:T(8,128)} %wv_ref.1), custom_call_target="tpu_custom_call" | custom-call | tf_op jit(solution)/shard_map/pallas_call | solution.py:569
  106.3 0.0 copy-start
  106.4 5.4 %bitcast_reduce_fusion = (f32[8,128]{1,0:T(8,128)S(1)}, f32[2048,128,8]{1,0,2:T(8,128)S(1)}) fusion(f32[2048,256]{1,0:T(8,128)} %bitcast.45, f32[128,1280]{1,0:T(8,128)} %get-tuple-element.8), kind=kOutput, calls=%fused_computation.3 | convolution fusion | flops 1614806016 | bytes 9965568 | tf_op jit(solution)/shard_map/rkgd,nkd->kgrn/dot_general | solution.py:40
  111.7 1.4 fusion.3
  113.1 0.0 copy-done
  113.1 3.7 %fusion.8 = f32[8,128,128]{1,2,0:T(8,128)S(1)} fusion(f32[2048,256]{1,0:T(8,128)S(1)} %bitcast.46, f32[2048,128,8]{1,0,2:T(8,128)S(1)} %get-tuple-element.10, f32[8,128]{1,0:T(8,128)S(1)} %broadcast_maximum_fusion, f32[8,128]{1,0:T(8,128)S(1)} %fusion.3), kind=kOutput, calls=%fused_computation.11 | convolution fusion | flops 1614938112 | bytes 9969664 | tf_op jit(solution)/shard_map/kgrn,nkd->kgrd/dot_general | solution.py:46
  116.8 1.0 copy.13.o_ref
  117.8 65.1 %shard_map.56 = f32[512,512]{1,0:T(8,128)} custom-call(f32[128,1024]{1,0:T(8,128)} %copy.13.o_ref, f32[1024,512]{1,0:T(8,128)} %wo_ref.1), custom_call_target="tpu_custom_call" | custom-call | tf_op jit(solution)/shard_map/pallas_call | solution.py:370
  182.9 2.3 %copy.22 = f32[512,512]{1,0:T(8,128)} copy(f32[512,512]{1,0:T(8,128)} %shard_map.56) | data formatting | bytes 2097152
  (1 shorter events, 0.0 us)
Async XLA Ops:
  106.3 6.8 %copy-start = (f32[8,16,16,256]{3,2,1,0:T(8,128)S(1)}, f32[8,16,16,256]{3,2,1,0:T(8,128)}, u32[]{:S(2)}) copy-start(f32[8,16,16,256]{3,2,1,0:T(8,128)} %get-tuple-element.7) | copy-start | bytes 6291460

commit v12 on v11

--- a/solution.py
+++ b/solution.py
@@ -592,19 +592,40 @@
     )(tokens, w_query, w_key, w_value)
 
 
+def attend_kernel(q_width, kv_width, q_ref, kv_ref, o_ref):
+    scale = 1.0 / math.sqrt(HEAD_SIZE_DIM)
+    keys = kv_ref[:, pl.ds(0, kv_width)]
+    values = kv_ref[:, pl.ds(kv_width, kv_width)]
+    for head in range(q_width // HEAD_SIZE_DIM):
+        query = q_ref[:, pl.ds(head * HEAD_SIZE_DIM, HEAD_SIZE_DIM)]
+        scores = lax.dot_general(
+            query, keys, (((1,), (1,)), ((), ())),
+            preferred_element_type=jnp.float32, precision=lax.Precision.HIGH,
+        ) * scale
+        weights = jnp.exp(scores - jnp.max(scores, axis=-1, keepdims=True))
+        total = jnp.sum(weights, axis=-1, keepdims=True)
+        weighted = jnp.dot(weights, values, preferred_element_type=jnp.float32, precision=lax.Precision.HIGH)
+        o_ref[:, pl.ds(head * HEAD_SIZE_DIM, HEAD_SIZE_DIM)] = weighted / total
+
+
+def attend(joined, all_kv, q_width, kv_width):
+    return pl.pallas_call(
+        functools.partial(attend_kernel, q_width, kv_width),
+        out_shape=jax.ShapeDtypeStruct((joined.shape[0], q_width), jnp.float32),
+        in_specs=[pl.BlockSpec(memory_space=pltpu.VMEM)] * 2,
+        out_specs=pl.BlockSpec(memory_space=pltpu.VMEM),
+        compiler_params=pltpu.CompilerParams(vmem_limit_bytes=60 * 1024 * 1024),
+    )(joined, all_kv)
+
+
 def on_device(ring, cols, tokens, w_query, w_key, w_value, w_out):
     highest = lax.Precision.HIGH
     q_width = w_query.shape[1]
     kv_width = w_key.shape[1]
     joined, kv_sets = front(tokens, w_query, w_key, w_value, ring, cols, 3)
-    query_rows = joined[:, :q_width]
     all_kv = kv_sets.reshape(-1, kv_sets.shape[-1])
-    state_end = fold_keys(
-        query_rows,
-        start_state(query_rows, kv_width),
-        (all_kv[:, :kv_width], all_kv[:, kv_width:]),
-    )
-    return gather_mix(finish(state_end), w_out, ring, cols, 5)
+    attended = attend(joined, all_kv, q_width, kv_width)
+    return gather_mix(attended, w_out, ring, cols, 5)
 
 
 def solution(mesh):

time: 187 us -> 187 us (level)
  Pallas kernels: 171 us -> 183 us
  matrix products: 9.05 us -> 0 us
    pallas_call x0 -> x1, Pallas kernels: none -> 11.4 us  [attend(): pl.pallas_call(functools.partial(attend_kernel, q_width, kv_width), out_s...]
    dot_general x2 -> x0, matrix products: 9.05 us -> none  [the longest x1 5.37 us: fold_keys(): jnp.einsum('rkgd,nkd->kgrn', query_head_rows, key_head_rows, precision=hi...]
where the time goes in v12:
time: 187 us; the launch traced here: 185 us
  Pallas kernels  183 us (98%)
  local copies, waits for them, and re-layouts  2.26 us (1%)
    pallas_call x1, Pallas kernels, front(): pl.pallas_call(functools.partial(front_kernel, ring, cols), out_shape=(ja...  106 us
    pallas_call x1, Pallas kernels, gather_mix(): pl.pallas_call(functools.partial(mix_kernel, ring, cols, n), out_shape=ja...  65.1 us
    pallas_call x1, Pallas kernels, attend(): pl.pallas_call(functools.partial(attend_kernel, q_width, kv_width), out_s...  11.4 us

profile of v12, /device:TPU:22, one launch (start us, length us, event | category | flops | bytes accessed | tf_op | source)
XLA Modules:
  0.0 185.1 jit_solution(17777102237794150756)
XLA Ops:
  0.0 106.3 %shard_map.55 = (f32[128,1280]{1,0:T(8,128)}, f32[8,16,16,256]{3,2,1,0:T(8,128)}) custom-call(f32[512,512]{1,0:T(8,128)} %tok_ref.1, f32[512,1024]{1,0:T(8,128)} %wq_ref.1, f32[512,128]{1,0:T(8,128)} %wk_ref.1, f32[512,128]{1,0:T(8,128)} %wv_ref.1), custom_call_target="tpu_custom_call" | custom-call | tf_op jit(solution)/shard_map/pallas_call | solution.py:569
  106.3 11.4 %shard_map.56.o_ref = f32[128,1024]{1,0:T(8,128)} custom-call(f32[128,1280]{1,0:T(8,128)} %get-tuple-element.7.q_ref, f32[2048,256]{1,0:T(8,128)} %bitcast.1), custom_call_target="tpu_custom_call" | custom-call | tf_op jit(solution)/shard_map/pallas_call | solution.py:612
  117.7 65.1 %shard_map.57 = f32[512,512]{1,0:T(8,128)} custom-call(f32[128,1024]{1,0:T(8,128)} %shard_map.56.o_ref, f32[1024,512]{1,0:T(8,128)} %wo_ref.1), custom_call_target="tpu_custom_call" | custom-call | tf_op jit(solution)/shard_map/pallas_call | solution.py:370
  182.8 2.3 %copy.7 = f32[512,512]{1,0:T(8,128)} copy(f32[512,512]{1,0:T(8,128)} %shard_map.57) | data formatting | bytes 2097152

commit v13 on v11

--- a/solution.py
+++ b/solution.py
@@ -253,7 +253,7 @@
     )(x)
 
 
-def mix_kernel(ring, cols, n, o_ref, wo_ref, out_ref, ogath, part, recv, send_sems, recv_sems, y_send, y_recv):
+def mix_kernel(ring, cols, n, o_ref, wo_ref, own_ref, out_ref, ogath, part, recv, send_sems, recv_sems, y_send, y_recv):
     mesh_id = pl.DeviceIdType.MESH
     names = ("depth", "rz", "rc", "col")
     me = {a: lax.axis_index(a) for a in names}
@@ -337,7 +337,8 @@
         cp.wait()
         project(ogath[slot(at, 1 - c)], slot(at, 1 - c))
     for k in range(2 * ring):
-        total = part[k, pl.ds(pl.multiple_of(y * piece, 8), piece)]
+        own = part[k, pl.ds(pl.multiple_of(y * piece, 8), piece)]
+        total = None
         for d in range(1, cols):
             pltpu.make_async_remote_copy(
                 src_ref=part.at[k, pl.ds(0, piece)],
@@ -347,10 +348,11 @@
                 device_id=device(col=lax.rem(y + d, cols)),
                 device_id_type=mesh_id,
             ).wait_recv()
-            total = total + recv[d, k]
+            total = recv[d, k] if total is None else total + recv[d, k]
         m = piece // 2
         for e in (0, 1):
             out_ref[pl.ds(e * 2 * ring * m + k * m, m)] = total[e * m : (e + 1) * m]
+            own_ref[pl.ds(e * 2 * ring * m + k * m, m)] = own[e * m : (e + 1) * m]
     for k in range(2 * ring):
         for d in range(1, cols):
             pltpu.make_async_remote_copy(
@@ -369,9 +371,12 @@
     per_col = 2 * ring // cols
     return pl.pallas_call(
         functools.partial(mix_kernel, ring, cols, n),
-        out_shape=jax.ShapeDtypeStruct((per_col * n, out_w), jnp.float32),
+        out_shape=(
+            jax.ShapeDtypeStruct((per_col * n, out_w), jnp.float32),
+            jax.ShapeDtypeStruct((per_col * n, out_w), jnp.float32),
+        ),
         in_specs=[pl.BlockSpec(memory_space=pltpu.VMEM), pl.BlockSpec(memory_space=pltpu.VMEM)],
-        out_specs=pl.BlockSpec(memory_space=pltpu.VMEM),
+        out_specs=(pl.BlockSpec(memory_space=pltpu.VMEM), pl.BlockSpec(memory_space=pltpu.VMEM)),
         scratch_shapes=[
             pltpu.VMEM((2 * ring, n, width), jnp.float32),
             pltpu.VMEM((2 * ring, n, out_w), jnp.float32),
@@ -604,7 +609,8 @@
         start_state(query_rows, kv_width),
         (all_kv[:, :kv_width], all_kv[:, kv_width:]),
     )
-    return gather_mix(finish(state_end), w_out, ring, cols, 5)
+    own, rest = gather_mix(finish(state_end), w_out, ring, cols, 5)
+    return own + rest
 
 
 def solution(mesh):

time: 187 us -> 188 us (level)
  other arithmetic: 1.37 us -> 4.09 us
  local copies, waits for them, and re-layouts: 3.26 us -> 1 us
    add x0 -> x1, other arithmetic: none -> 2.72 us  [on_device(): return own + rest]
    unnamed x3 -> x2, local copies, waits for them, and re-layouts: 2.27 us -> 0.01 us
where the time goes in v13:
time: 188 us; the launch traced here: 186 us
  Pallas kernels  172 us (91%)
  matrix products  9.05 us (5%)
  other arithmetic  4.09 us (2%)
    pallas_call x1, Pallas kernels, front(): pl.pallas_call(functools.partial(front_kernel, ring, cols), out_shape=(ja...  106 us
    pallas_call x1, Pallas kernels, gather_mix(): pl.pallas_call(functools.partial(mix_kernel, ring, cols, n), out_shape=(j...  65.5 us
    dot_general x1, matrix products, fold_keys(): jnp.einsum('rkgd,nkd->kgrn', query_head_rows, key_head_rows, precision=hi...  5.37 us

profile of v13, /device:TPU:22, one launch (start us, length us, event | category | flops | bytes accessed | tf_op | source)
XLA Modules:
  0.0 186.0 jit_solution(17521781598618763666)
XLA Ops:
  0.0 106.3 %shard_map.55 = (f32[128,1280]{1,0:T(8,128)}, f32[8,16,16,256]{3,2,1,0:T(8,128)}) custom-call(f32[512,512]{1,0:T(8,128)} %tok_ref.1, f32[512,1024]{1,0:T(8,128)} %wq_ref.1, f32[512,128]{1,0:T(8,128)} %wk_ref.1, f32[512,128]{1,0:T(8,128)} %wv_ref.1), custom_call_target="tpu_custom_call" | custom-call | tf_op jit(solution)/shard_map/pallas_call | solution.py:574
  106.3 0.0 copy-start
  106.4 5.4 %bitcast_reduce_fusion = (f32[8,128]{1,0:T(8,128)S(1)}, f32[2048,128,8]{1,0,2:T(8,128)S(1)}) fusion(f32[2048,256]{1,0:T(8,128)} %bitcast.45, f32[128,1280]{1,0:T(8,128)} %get-tuple-element.10), kind=kOutput, calls=%fused_computation.3 | convolution fusion | flops 1614806016 | bytes 9965568 | tf_op jit(solution)/shard_map/rkgd,nkd->kgrn/dot_general | solution.py:40
  111.7 1.4 fusion.3
  113.1 0.0 copy-done
  113.1 3.7 %fusion.8 = f32[8,128,128]{1,2,0:T(8,128)S(1)} fusion(f32[2048,256]{1,0:T(8,128)S(1)} %bitcast.46, f32[2048,128,8]{1,0,2:T(8,128)S(1)} %get-tuple-element.14, f32[8,128]{1,0:T(8,128)S(1)} %broadcast_maximum_fusion, f32[8,128]{1,0:T(8,128)S(1)} %fusion.3), kind=kOutput, calls=%fused_computation.11 | convolution fusion | flops 1614938112 | bytes 9969664 | tf_op jit(solution)/shard_map/kgrn,nkd->kgrd/dot_general | solution.py:46
  116.8 1.0 copy.13.o_ref
  117.8 65.5 %shard_map.56 = (f32[512,512]{1,0:T(8,128)}, f32[512,512]{1,0:T(8,128)}) custom-call(f32[128,1024]{1,0:T(8,128)} %copy.13.o_ref, f32[1024,512]{1,0:T(8,128)} %wo_ref.1), custom_call_target="tpu_custom_call" | custom-call | tf_op jit(solution)/shard_map/pallas_call | solution.py:372
  183.3 2.7 %add.3 = f32[512,512]{1,0:T(8,128)} add(f32[512,512]{1,0:T(8,128)} %get-tuple-element.11, f32[512,512]{1,0:T(8,128)} %get-tuple-element.12) | non-fusion elementwise | flops 262144 | bytes 3145728 | tf_op jit(solution)/shard_map/add | solution.py:613
  (1 shorter events, 0.0 us)
Async XLA Ops:
  106.3 6.8 %copy-start = (f32[8,16,16,256]{3,2,1,0:T(8,128)S(1)}, f32[8,16,16,256]{3,2,1,0:T(8,128)}, u32[]{:S(2)}) copy-start(f32[8,16,16,256]{3,2,1,0:T(8,128)} %get-tuple-element.9) | copy-start | bytes 6291460

commit v14 on v11

--- a/solution.py
+++ b/solution.py
@@ -536,7 +536,7 @@
 
     begin(0, 0, sub(tok_ref, 0))
     begin(0, 1, sub(tok_ref, 1))
-    advance(ring // 2)
+    advance(ring - 1)
     y1[("r", 0)].wait()
     y2r = remote(sub(tg.at[1], 0), sub(tg.at[3], 0), y_right, y_sems, 4)
     y1[("l", 0)].wait()

time: 187 us -> 193 us (1.032)
  Pallas kernels: 171 us -> 178 us
    pallas_call x1, Pallas kernels: 106 us -> 113 us  [front(): pl.pallas_call(functools.partial(front_kernel, ring, cols), out_shape=(ja...]
where the time goes in v14:
time: 193 us; the launch traced here: 192 us
  Pallas kernels  178 us (92%)
  matrix products  9.05 us (5%)
  local copies, waits for them, and re-layouts  3.26 us (2%)
    pallas_call x1, Pallas kernels, front(): pl.pallas_call(functools.partial(front_kernel, ring, cols), out_shape=(ja...  113 us
    pallas_call x1, Pallas kernels, gather_mix(): pl.pallas_call(functools.partial(mix_kernel, ring, cols, n), out_shape=ja...  64.8 us
    dot_general x1, matrix products, fold_keys(): jnp.einsum('rkgd,nkd->kgrn', query_head_rows, key_head_rows, precision=hi...  5.37 us

profile of v14, /device:TPU:22, one launch (start us, length us, event | category | flops | bytes accessed | tf_op | source)
XLA Modules:
  0.0 191.7 jit_solution(12783479511733694830)
XLA Ops:
  0.0 113.1 %shard_map.55 = (f32[128,1280]{1,0:T(8,128)}, f32[8,16,16,256]{3,2,1,0:T(8,128)}) custom-call(f32[512,512]{1,0:T(8,128)} %tok_ref.1, f32[512,1024]{1,0:T(8,128)} %wq_ref.1, f32[512,128]{1,0:T(8,128)} %wk_ref.1, f32[512,128]{1,0:T(8,128)} %wv_ref.1), custom_call_target="tpu_custom_call" | custom-call | tf_op jit(solution)/shard_map/pallas_call | solution.py:569
  113.2 0.0 copy-start
  113.2 5.4 %bitcast_reduce_fusion = (f32[8,128]{1,0:T(8,128)S(1)}, f32[2048,128,8]{1,0,2:T(8,128)S(1)}) fusion(f32[2048,256]{1,0:T(8,128)} %bitcast.45, f32[128,1280]{1,0:T(8,128)} %get-tuple-element.8), kind=kOutput, calls=%fused_computation.3 | convolution fusion | flops 1614806016 | bytes 9965568 | tf_op jit(solution)/shard_map/rkgd,nkd->kgrn/dot_general | solution.py:40
  118.6 1.4 fusion.3
  119.9 0.0 copy-done
  119.9 3.7 %fusion.8 = f32[8,128,128]{1,2,0:T(8,128)S(1)} fusion(f32[2048,256]{1,0:T(8,128)S(1)} %bitcast.46, f32[2048,128,8]{1,0,2:T(8,128)S(1)} %get-tuple-element.10, f32[8,128]{1,0:T(8,128)S(1)} %broadcast_maximum_fusion, f32[8,128]{1,0:T(8,128)S(1)} %fusion.3), kind=kOutput, calls=%fused_computation.11 | convolution fusion | flops 1614938112 | bytes 9969664 | tf_op jit(solution)/shard_map/kgrn,nkd->kgrd/dot_general | solution.py:46
  123.6 1.0 copy.13.o_ref
  124.6 64.8 %shard_map.56 = f32[512,512]{1,0:T(8,128)} custom-call(f32[128,1024]{1,0:T(8,128)} %copy.13.o_ref, f32[1024,512]{1,0:T(8,128)} %wo_ref.1), custom_call_target="tpu_custom_call" | custom-call | tf_op jit(solution)/shard_map/pallas_call | solution.py:370
  189.4 2.3 %copy.22 = f32[512,512]{1,0:T(8,128)} copy(f32[512,512]{1,0:T(8,128)} %shard_map.56) | data formatting | bytes 2097152
  (1 shorter events, 0.0 us)
Async XLA Ops:
  113.2 6.8 %copy-start = (f32[8,16,16,256]{3,2,1,0:T(8,128)S(1)}, f32[8,16,16,256]{3,2,1,0:T(8,128)}, u32[]{:S(2)}) copy-start(f32[8,16,16,256]{3,2,1,0:T(8,128)} %get-tuple-element.7) | copy-start | bytes 6291460

commit v15 on v14

--- a/solution.py
+++ b/solution.py
@@ -536,7 +536,7 @@
 
     begin(0, 0, sub(tok_ref, 0))
     begin(0, 1, sub(tok_ref, 1))
-    advance(ring - 1)
+    advance(2)
     y1[("r", 0)].wait()
     y2r = remote(sub(tg.at[1], 0), sub(tg.at[3], 0), y_right, y_sems, 4)
     y1[("l", 0)].wait()

time: 193 us -> 189 us (0.979)
  Pallas kernels: 178 us -> 173 us
    pallas_call x1, Pallas kernels: 113 us -> 109 us  [front(): pl.pallas_call(functools.partial(front_kernel, ring, cols), out_shape=(ja...]
where the time goes in v15:
time: 189 us; the launch traced here: 187 us
  Pallas kernels  173 us (92%)
  matrix products  9.05 us (5%)
  local copies, waits for them, and re-layouts  3.26 us (2%)
    pallas_call x1, Pallas kernels, front(): pl.pallas_call(functools.partial(front_kernel, ring, cols), out_shape=(ja...  109 us
    pallas_call x1, Pallas kernels, gather_mix(): pl.pallas_call(functools.partial(mix_kernel, ring, cols, n), out_shape=ja...  64.5 us
    dot_general x1, matrix products, fold_keys(): jnp.einsum('rkgd,nkd->kgrn', query_head_rows, key_head_rows, precision=hi...  5.37 us

profile of v15, /device:TPU:22, one launch (start us, length us, event | category | flops | bytes accessed | tf_op | source)
XLA Modules:
  0.0 187.1 jit_solution(15298949551742096721)
XLA Ops:
  0.0 108.9 %shard_map.55 = (f32[128,1280]{1,0:T(8,128)}, f32[8,16,16,256]{3,2,1,0:T(8,128)}) custom-call(f32[512,512]{1,0:T(8,128)} %tok_ref.1, f32[512,1024]{1,0:T(8,128)} %wq_ref.1, f32[512,128]{1,0:T(8,128)} %wk_ref.1, f32[512,128]{1,0:T(8,128)} %wv_ref.1), custom_call_target="tpu_custom_call" | custom-call | tf_op jit(solution)/shard_map/pallas_call | solution.py:569
  108.9 0.0 copy-start
  108.9 5.4 %bitcast_reduce_fusion = (f32[8,128]{1,0:T(8,128)S(1)}, f32[2048,128,8]{1,0,2:T(8,128)S(1)}) fusion(f32[2048,256]{1,0:T(8,128)} %bitcast.45, f32[128,1280]{1,0:T(8,128)} %get-tuple-element.8), kind=kOutput, calls=%fused_computation.3 | convolution fusion | flops 1614806016 | bytes 9965568 | tf_op jit(solution)/shard_map/rkgd,nkd->kgrn/dot_general | solution.py:40
  114.3 1.4 fusion.3
  115.7 0.0 copy-done
  115.7 3.7 %fusion.8 = f32[8,128,128]{1,2,0:T(8,128)S(1)} fusion(f32[2048,256]{1,0:T(8,128)S(1)} %bitcast.46, f32[2048,128,8]{1,0,2:T(8,128)S(1)} %get-tuple-element.10, f32[8,128]{1,0:T(8,128)S(1)} %broadcast_maximum_fusion, f32[8,128]{1,0:T(8,128)S(1)} %fusion.3), kind=kOutput, calls=%fused_computation.11 | convolution fusion | flops 1614938112 | bytes 9969664 | tf_op jit(solution)/shard_map/kgrn,nkd->kgrd/dot_general | solution.py:46
  119.4 1.0 copy.13.o_ref
  120.4 64.5 %shard_map.56 = f32[512,512]{1,0:T(8,128)} custom-call(f32[128,1024]{1,0:T(8,128)} %copy.13.o_ref, f32[1024,512]{1,0:T(8,128)} %wo_ref.1), custom_call_target="tpu_custom_call" | custom-call | tf_op jit(solution)/shard_map/pallas_call | solution.py:370
  184.9 2.3 %copy.22 = f32[512,512]{1,0:T(8,128)} copy(f32[512,512]{1,0:T(8,128)} %shard_map.56) | data formatting | bytes 2097152
  (1 shorter events, 0.0 us)
Async XLA Ops:
  108.9 6.8 %copy-start = (f32[8,16,16,256]{3,2,1,0:T(8,128)S(1)}, f32[8,16,16,256]{3,2,1,0:T(8,128)}, u32[]{:S(2)}) copy-start(f32[8,16,16,256]{3,2,1,0:T(8,128)} %get-tuple-element.7) | copy-start | bytes 6291460

commit v16 on v11

--- a/solution.py
+++ b/solution.py
@@ -542,7 +542,7 @@
     y1[("l", 0)].wait()
     begin(1, 0, sub(tg.at[1], 0))
     begin(2, 0, sub(tg.at[2], 0))
-    advance(2)
+    advance(3)
     y1[("r", 1)].wait()
     y1[("l", 1)].wait()
     y2l = remote(sub(tg.at[2], 1), sub(tg.at[3], 1), y_left, y_sems, 5)

time: 187 us -> 185 us (0.989)
  no operation moved by 1% of the time
where the time goes in v16:
time: 185 us; the launch traced here: 184 us
  Pallas kernels  170 us (92%)
  matrix products  9.05 us (5%)
  local copies, waits for them, and re-layouts  3.26 us (2%)
    pallas_call x1, Pallas kernels, front(): pl.pallas_call(functools.partial(front_kernel, ring, cols), out_shape=(ja...  106 us
    pallas_call x1, Pallas kernels, gather_mix(): pl.pallas_call(functools.partial(mix_kernel, ring, cols, n), out_shape=ja...  64.5 us
    dot_general x1, matrix products, fold_keys(): jnp.einsum('rkgd,nkd->kgrn', query_head_rows, key_head_rows, precision=hi...  5.37 us

profile of v16, /device:TPU:22, one launch (start us, length us, event | category | flops | bytes accessed | tf_op | source)
XLA Modules:
  0.0 183.8 jit_solution(8029113624896701508)
XLA Ops:
  0.0 105.6 %shard_map.55 = (f32[128,1280]{1,0:T(8,128)}, f32[8,16,16,256]{3,2,1,0:T(8,128)}) custom-call(f32[512,512]{1,0:T(8,128)} %tok_ref.1, f32[512,1024]{1,0:T(8,128)} %wq_ref.1, f32[512,128]{1,0:T(8,128)} %wk_ref.1, f32[512,128]{1,0:T(8,128)} %wv_ref.1), custom_call_target="tpu_custom_call" | custom-call | tf_op jit(solution)/shard_map/pallas_call | solution.py:569
  105.6 0.0 copy-start
  105.6 5.4 %bitcast_reduce_fusion = (f32[8,128]{1,0:T(8,128)S(1)}, f32[2048,128,8]{1,0,2:T(8,128)S(1)}) fusion(f32[2048,256]{1,0:T(8,128)} %bitcast.45, f32[128,1280]{1,0:T(8,128)} %get-tuple-element.8), kind=kOutput, calls=%fused_computation.3 | convolution fusion | flops 1614806016 | bytes 9965568 | tf_op jit(solution)/shard_map/rkgd,nkd->kgrn/dot_general | solution.py:40
  111.0 1.4 fusion.3
  112.3 0.0 copy-done
  112.4 3.7 %fusion.8 = f32[8,128,128]{1,2,0:T(8,128)S(1)} fusion(f32[2048,256]{1,0:T(8,128)S(1)} %bitcast.46, f32[2048,128,8]{1,0,2:T(8,128)S(1)} %get-tuple-element.10, f32[8,128]{1,0:T(8,128)S(1)} %broadcast_maximum_fusion, f32[8,128]{1,0:T(8,128)S(1)} %fusion.3), kind=kOutput, calls=%fused_computation.11 | convolution fusion | flops 1614938112 | bytes 9969664 | tf_op jit(solution)/shard_map/kgrn,nkd->kgrd/dot_general | solution.py:46
  116.0 1.0 copy.13.o_ref
  117.0 64.5 %shard_map.56 = f32[512,512]{1,0:T(8,128)} custom-call(f32[128,1024]{1,0:T(8,128)} %copy.13.o_ref, f32[1024,512]{1,0:T(8,128)} %wo_ref.1), custom_call_target="tpu_custom_call" | custom-call | tf_op jit(solution)/shard_map/pallas_call | solution.py:370
  181.5 2.3 %copy.22 = f32[512,512]{1,0:T(8,128)} copy(f32[512,512]{1,0:T(8,128)} %shard_map.56) | data formatting | bytes 2097152
  (1 shorter events, 0.0 us)
Async XLA Ops:
  105.6 6.8 %copy-start = (f32[8,16,16,256]{3,2,1,0:T(8,128)S(1)}, f32[8,16,16,256]{3,2,1,0:T(8,128)}, u32[]{:S(2)}) copy-start(f32[8,16,16,256]{3,2,1,0:T(8,128)} %get-tuple-element.7) | copy-start | bytes 6291460

commit v17 on v16

--- a/solution.py
+++ b/solution.py
@@ -548,7 +548,7 @@
     y2l = remote(sub(tg.at[2], 1), sub(tg.at[3], 1), y_left, y_sems, 5)
     begin(1, 1, sub(tg.at[1], 1))
     begin(2, 1, sub(tg.at[2], 1))
-    advance(2)
+    advance(3)
     y2r.wait()
     begin(3, 0, sub(tg.at[3], 0))
     y2l.wait()

time: 185 us -> 188 us (1.016)
  Pallas kernels: 170 us -> 172 us
where the time goes in v17:
time: 188 us; the launch traced here: 186 us
  Pallas kernels  172 us (91%)
  matrix products  9.06 us (5%)
  local copies, waits for them, and re-layouts  3.26 us (2%)
    pallas_call x1, Pallas kernels, front(): pl.pallas_call(functools.partial(front_kernel, ring, cols), out_shape=(ja...  107 us
    pallas_call x1, Pallas kernels, gather_mix(): pl.pallas_call(functools.partial(mix_kernel, ring, cols, n), out_shape=ja...  64.6 us
    dot_general x1, matrix products, fold_keys(): jnp.einsum('rkgd,nkd->kgrn', query_head_rows, key_head_rows, precision=hi...  5.37 us

profile of v17, /device:TPU:22, one launch (start us, length us, event | category | flops | bytes accessed | tf_op | source)
XLA Modules:
  0.0 185.6 jit_solution(9537585925751804391)
XLA Ops:
  0.0 107.3 %shard_map.55 = (f32[128,1280]{1,0:T(8,128)}, f32[8,16,16,256]{3,2,1,0:T(8,128)}) custom-call(f32[512,512]{1,0:T(8,128)} %tok_ref.1, f32[512,1024]{1,0:T(8,128)} %wq_ref.1, f32[512,128]{1,0:T(8,128)} %wk_ref.1, f32[512,128]{1,0:T(8,128)} %wv_ref.1), custom_call_target="tpu_custom_call" | custom-call | tf_op jit(solution)/shard_map/pallas_call | solution.py:569
  107.3 0.0 copy-start
  107.3 5.4 %bitcast_reduce_fusion = (f32[8,128]{1,0:T(8,128)S(1)}, f32[2048,128,8]{1,0,2:T(8,128)S(1)}) fusion(f32[2048,256]{1,0:T(8,128)} %bitcast.45, f32[128,1280]{1,0:T(8,128)} %get-tuple-element.8), kind=kOutput, calls=%fused_computation.3 | convolution fusion | flops 1614806016 | bytes 9965568 | tf_op jit(solution)/shard_map/rkgd,nkd->kgrn/dot_general | solution.py:40
  112.7 1.4 fusion.3
  114.1 0.0 copy-done
  114.1 3.7 %fusion.8 = f32[8,128,128]{1,2,0:T(8,128)S(1)} fusion(f32[2048,256]{1,0:T(8,128)S(1)} %bitcast.46, f32[2048,128,8]{1,0,2:T(8,128)S(1)} %get-tuple-element.10, f32[8,128]{1,0:T(8,128)S(1)} %broadcast_maximum_fusion, f32[8,128]{1,0:T(8,128)S(1)} %fusion.3), kind=kOutput, calls=%fused_computation.11 | convolution fusion | flops 1614938112 | bytes 9969664 | tf_op jit(solution)/shard_map/kgrn,nkd->kgrd/dot_general | solution.py:46
  117.8 1.0 copy.13.o_ref
  118.8 64.6 %shard_map.56 = f32[512,512]{1,0:T(8,128)} custom-call(f32[128,1024]{1,0:T(8,128)} %copy.13.o_ref, f32[1024,512]{1,0:T(8,128)} %wo_ref.1), custom_call_target="tpu_custom_call" | custom-call | tf_op jit(solution)/shard_map/pallas_call | solution.py:370
  183.4 2.3 %copy.22 = f32[512,512]{1,0:T(8,128)} copy(f32[512,512]{1,0:T(8,128)} %shard_map.56) | data formatting | bytes 2097152
  (1 shorter events, 0.0 us)
Async XLA Ops:
  107.3 6.8 %copy-start = (f32[8,16,16,256]{3,2,1,0:T(8,128)S(1)}, f32[8,16,16,256]{3,2,1,0:T(8,128)}, u32[]{:S(2)}) copy-start(f32[8,16,16,256]{3,2,1,0:T(8,128)} %get-tuple-element.7) | copy-start | bytes 6291460

commit v18 on v16

--- a/solution.py
+++ b/solution.py
@@ -542,7 +542,7 @@
     y1[("l", 0)].wait()
     begin(1, 0, sub(tg.at[1], 0))
     begin(2, 0, sub(tg.at[2], 0))
-    advance(3)
+    advance(4)
     y1[("r", 1)].wait()
     y1[("l", 1)].wait()
     y2l = remote(sub(tg.at[2], 1), sub(tg.at[3], 1), y_left, y_sems, 5)

time: 185 us -> 187 us (1.011)
  Pallas kernels: 170 us -> 172 us
    pallas_call x1, Pallas kernels: 106 us -> 108 us  [front(): pl.pallas_call(functools.partial(front_kernel, ring, cols), out_shape=(ja...]
where the time goes in v18:
time: 187 us; the launch traced here: 186 us
  Pallas kernels  172 us (92%)
  matrix products  9.05 us (5%)
  local copies, waits for them, and re-layouts  3.26 us (2%)
    pallas_call x1, Pallas kernels, front(): pl.pallas_call(functools.partial(front_kernel, ring, cols), out_shape=(ja...  108 us
    pallas_call x1, Pallas kernels, gather_mix(): pl.pallas_call(functools.partial(mix_kernel, ring, cols, n), out_shape=ja...  64.4 us
    dot_general x1, matrix products, fold_keys(): jnp.einsum('rkgd,nkd->kgrn', query_head_rows, key_head_rows, precision=hi...  5.37 us

profile of v18, /device:TPU:22, one launch (start us, length us, event | category | flops | bytes accessed | tf_op | source)
XLA Modules:
  0.0 185.8 jit_solution(10858589308643744543)
XLA Ops:
  0.0 107.6 %shard_map.55 = (f32[128,1280]{1,0:T(8,128)}, f32[8,16,16,256]{3,2,1,0:T(8,128)}) custom-call(f32[512,512]{1,0:T(8,128)} %tok_ref.1, f32[512,1024]{1,0:T(8,128)} %wq_ref.1, f32[512,128]{1,0:T(8,128)} %wk_ref.1, f32[512,128]{1,0:T(8,128)} %wv_ref.1), custom_call_target="tpu_custom_call" | custom-call | tf_op jit(solution)/shard_map/pallas_call | solution.py:569
  107.7 0.0 copy-start
  107.7 5.4 %bitcast_reduce_fusion = (f32[8,128]{1,0:T(8,128)S(1)}, f32[2048,128,8]{1,0,2:T(8,128)S(1)}) fusion(f32[2048,256]{1,0:T(8,128)} %bitcast.45, f32[128,1280]{1,0:T(8,128)} %get-tuple-element.8), kind=kOutput, calls=%fused_computation.3 | convolution fusion | flops 1614806016 | bytes 9965568 | tf_op jit(solution)/shard_map/rkgd,nkd->kgrn/dot_general | solution.py:40
  113.1 1.4 fusion.3
  114.4 0.0 copy-done
  114.4 3.7 %fusion.8 = f32[8,128,128]{1,2,0:T(8,128)S(1)} fusion(f32[2048,256]{1,0:T(8,128)S(1)} %bitcast.46, f32[2048,128,8]{1,0,2:T(8,128)S(1)} %get-tuple-element.10, f32[8,128]{1,0:T(8,128)S(1)} %broadcast_maximum_fusion, f32[8,128]{1,0:T(8,128)S(1)} %fusion.3), kind=kOutput, calls=%fused_computation.11 | convolution fusion | flops 1614938112 | bytes 9969664 | tf_op jit(solution)/shard_map/kgrn,nkd->kgrd/dot_general | solution.py:46
  118.1 1.0 copy.13.o_ref
  119.1 64.4 %shard_map.56 = f32[512,512]{1,0:T(8,128)} custom-call(f32[128,1024]{1,0:T(8,128)} %copy.13.o_ref, f32[1024,512]{1,0:T(8,128)} %wo_ref.1), custom_call_target="tpu_custom_call" | custom-call | tf_op jit(solution)/shard_map/pallas_call | solution.py:370
  183.5 2.3 %copy.22 = f32[512,512]{1,0:T(8,128)} copy(f32[512,512]{1,0:T(8,128)} %shard_map.56) | data formatting | bytes 2097152
  (1 shorter events, 0.0 us)
Async XLA Ops:
  107.7 6.8 %copy-start = (f32[8,16,16,256]{3,2,1,0:T(8,128)S(1)}, f32[8,16,16,256]{3,2,1,0:T(8,128)}, u32[]{:S(2)}) copy-start(f32[8,16,16,256]{3,2,1,0:T(8,128)} %get-tuple-element.7) | copy-start | bytes 6291460
